TPU v7x, 32 devices: a whole 2x2x4 slice. The times are simulated.
32 devices in a mesh: dom: 16 (over z, y, core), rep: 2 (over x).
Axes of the slice: x: 2, y: 2, z: 4, core: 2. Of those that a mesh axis runs over, the one named last changes fastest.
Arguments:
- node_feats: bfloat16 [4096, 400], P('dom'), may hold values from -6 to 6
- w_self: bfloat16 [400, 400], replicated, may hold values from -0.3125 to 0.3125
- w_neigh: bfloat16 [400, 400], replicated, may hold values from -0.3125 to 0.3125
- neighbour_index: int32 [4096, 10], P('dom'), may hold values from 0 to 383, as said below
- neighbour_count: int32 [4096], P('dom'), may hold values from 1 to 10
- send_index: int32 [16, 16, 8], P('dom'), may hold values from 0 to 255
- send_count: int32 [16, 16], P('dom'), may hold values from 0 to 8
- edge_src: int32 [16, 5, 512], P('dom', None, 'rep'), may hold values from 0 to 255
- edge_dst: int32 [16, 5, 512], P('dom', None, 'rep'), may hold values from 0 to 255
- tile_count: int32 [16, 5, 4], P('dom', None, 'rep'), may hold values from 1 to 128, as said below
- neg_rows: int32 [16, 5, 512], P('dom'), may hold values from 0 to 255
Outputs:
- loss: float32 [], replicated
- grad_x: float32 [4096, 400], P('dom')
- grad_self: float32 [400, 400], replicated
- grad_neigh: float32 [400, 400], replicated
Inputs may be any that keep to these rules, and one draw needn't show every extreme that they name: `neighbour_index`: a value below 256 is a node of the own partition; a value 256 + s * 8 + c is slot c of sender s, which holds zeros when c >= send_count[s, p]; slots at or beyond neighbour_count are ignored. `tile_count`: every bucket has at least one full tile.
All inputs are finite; a program needn't handle non-finite values.
Results may differ from a plain program's by a relative error of at most 0.0035.
Values may be sent and summed in bfloat16 or wider, within the bound.
A program may use at most 64 MiB of HBM per device.

v0:
```python
import jax
import jax.numpy as jnp
from jax import lax
from jax.sharding import PartitionSpec as P

negative_weight = 0.03125


def from_behind(value, axis, steps):
    count = lax.axis_size(axis)
    pairs = [(source, (source + steps) % count) for source in range(count)]
    return lax.ppermute(value, axis, pairs)


def edge_terms(own, visitor, sources, targets, filled, negatives):
    edge_total = sources.shape[0]
    scale = own.shape[1] ** (-0.5)
    position = jnp.arange(edge_total, dtype=jnp.int32)
    live = (position % 128 < jnp.repeat(filled, 128, total_repeat_length=edge_total)).astype(
        jnp.float32
    )
    src_emb = own[sources]
    dst_emb = visitor[targets]
    neg_emb = visitor[negatives]
    positive = jnp.sum(src_emb.astype(jnp.float32) * dst_emb.astype(jnp.float32), axis=1) * scale
    negative = (
        lax.dot_general(
            src_emb, neg_emb, (((1,), (1,)), ((), ())), preferred_element_type=jnp.float32
        )
        * scale
    )
    loss_part = jnp.sum(
        live
        * (
            jax.nn.softplus(-positive)
            + negative_weight * jnp.sum(jax.nn.softplus(negative), axis=1)
        )
    )
    pos_grad = -live * jax.nn.sigmoid(-positive)
    neg_grad = (live[:, None] * negative_weight * jax.nn.sigmoid(negative)).astype(jnp.bfloat16)
    src_grad = scale * (
        pos_grad[:, None] * dst_emb.astype(jnp.float32)
        + jnp.dot(neg_grad, neg_emb, preferred_element_type=jnp.float32)
    )
    dst_grad = scale * pos_grad[:, None] * src_emb.astype(jnp.float32)
    neg_back = scale * lax.dot_general(
        neg_grad, src_emb, (((0,), (0,)), ((), ())), preferred_element_type=jnp.float32
    )
    home = jnp.zeros(own.shape, jnp.float32).at[sources].add(src_grad)
    visiting = (
        jnp.zeros(visitor.shape, jnp.float32).at[targets].add(dst_grad).at[negatives].add(neg_back)
    )
    return (loss_part, home, visiting)


def on_device(
    node_feats,
    w_self,
    w_neigh,
    neighbour_index,
    neighbour_count,
    send_index,
    send_count,
    edge_src,
    edge_dst,
    tile_count,
    neg_rows,
):
    partitions = lax.axis_size("dom")
    replicas = lax.axis_size("rep")
    node_rows, width = node_feats.shape
    fan_out = neighbour_index.shape[1]
    slot_cap = send_index.shape[2]
    window = edge_src.shape[1]
    half_width = (window - 1) // 2
    edge_here = edge_src.shape[2]
    tiles_here = tile_count.shape[2]
    sent_rows = send_index[0]
    slot_live = jnp.arange(slot_cap, dtype=jnp.int32)[None, :] < send_count[0][:, None]
    outgoing = jnp.where(slot_live[:, :, None], node_feats[sent_rows], jnp.zeros((), jnp.bfloat16))
    incoming = lax.all_to_all(outgoing, "dom", split_axis=0, concat_axis=0, tiled=True)
    lookup_table = jnp.concatenate(
        [node_feats, incoming.reshape(partitions * slot_cap, width)], axis=0
    )
    columns = jnp.arange(lookup_table.shape[0], dtype=jnp.int32)
    counts_f = neighbour_count.astype(jnp.float32)[:, None]
    adjacency = jnp.zeros((node_rows, lookup_table.shape[0]), jnp.bfloat16)
    for which in range(fan_out):
        hits = (neighbour_index[:, which : which + 1] == columns[None, :]) & (
            which < neighbour_count
        )[:, None]
        adjacency = adjacency + hits.astype(jnp.bfloat16)
    neighbour_mean = (
        jnp.dot(adjacency, lookup_table, preferred_element_type=jnp.float32) / counts_f
    ).astype(jnp.bfloat16)
    hidden = (
        jnp.dot(node_feats, w_self, preferred_element_type=jnp.float32)
        + jnp.dot(neighbour_mean, w_neigh, preferred_element_type=jnp.float32)
    ).astype(jnp.bfloat16)
    home = jnp.zeros((node_rows, width), jnp.float32)
    loss_sum = jnp.zeros((), jnp.float32)
    visitor = from_behind(hidden, "dom", -half_width)
    for step in range(window):
        offset = half_width - step
        visit_slot = offset + half_width
        part_loss, home_part, block_part = edge_terms(
            hidden,
            visitor,
            edge_src[0, visit_slot],
            edge_dst[0, visit_slot],
            tile_count[0, visit_slot],
            neg_rows[0, visit_slot],
        )
        loss_sum = loss_sum + part_loss
        home = home + home_part
        if offset == 0:
            home = home + block_part
        else:
            slot = half_width - offset
            packed = jnp.concatenate(
                [edge_src[0, slot], edge_dst[0, slot], tile_count[0, slot], neg_rows[0, slot]],
                axis=0,
            )
            moved = from_behind(packed, "dom", -offset)
            sources = moved[:edge_here]
            targets = moved[edge_here : 2 * edge_here]
            filled = moved[2 * edge_here : 2 * edge_here + tiles_here]
            negatives = moved[2 * edge_here + tiles_here :]
            unused_loss, unused_home, visiting = edge_terms(
                visitor, hidden, sources, targets, filled, negatives
            )
            home = home + visiting
        if step + 1 < window:
            visitor = from_behind(visitor, "dom", 1)
    home_total, loss_total = lax.psum((home, loss_sum), "rep")
    grad_b = home_total.astype(jnp.bfloat16)
    direct = lax.dot_general(
        grad_b, w_self, (((1,), (1,)), ((), ())), preferred_element_type=jnp.float32
    )
    grad_mean = (
        lax.dot_general(
            grad_b, w_neigh, (((1,), (1,)), ((), ())), preferred_element_type=jnp.float32
        )
        / counts_f
    ).astype(jnp.bfloat16)
    table_grad = lax.dot_general(
        adjacency, grad_mean, (((0,), (0,)), ((), ())), preferred_element_type=jnp.float32
    )
    remote_grad = table_grad[node_rows:].reshape(partitions, slot_cap, width)
    returned = lax.all_to_all(
        remote_grad.astype(jnp.bfloat16), "dom", split_axis=0, concat_axis=0, tiled=True
    ).astype(remote_grad.dtype)
    returned = jnp.where(slot_live[:, :, None], returned, jnp.zeros((), jnp.float32))
    scattered = (
        jnp.zeros((node_rows, width), jnp.float32)
        .at[sent_rows.reshape(-1)]
        .add(returned.reshape(partitions * slot_cap, width))
    )
    grad_x = direct + table_grad[:node_rows] + scattered
    scale = float(node_rows * partitions) ** (-0.5)
    self_part = (
        lax.dot_general(
            node_feats, grad_b, (((0,), (0,)), ((), ())), preferred_element_type=jnp.float32
        )
        * scale
    )
    neigh_part = (
        lax.dot_general(
            neighbour_mean, grad_b, (((0,), (0,)), ((), ())), preferred_element_type=jnp.float32
        )
        * scale
    )
    grad_self, grad_neigh, loss_all = lax.psum((self_part, neigh_part, loss_total), "dom")
    loss = loss_all / float(partitions * window * edge_here * replicas)
    return (loss, grad_x, grad_self, grad_neigh)


def solution(mesh):
    in_specs = (
        P("dom", None),
        P(),
        P(),
        P("dom", None),
        P("dom"),
        P("dom", None, None),
        P("dom", None),
        P("dom", None, "rep"),
        P("dom", None, "rep"),
        P("dom", None, "rep"),
        P("dom", None, None),
    )
    out_specs = (P(), P("dom", None), P(), P())
    return jax.shard_map(
        on_device, mesh=mesh, in_specs=in_specs, out_specs=out_specs, check_vma=False
    )
```

profile of v0, /device:TPU:0, one launch (start us, length us, event | category | flops | bytes accessed | tf_op | source)
XLA Modules:
  0.0 344.6 jit_solution(11012656341770856391)
XLA Ops:
  10.9 7.5 %all-to-all-start = ((bf16[16,8,400]{2,1,0:T(8,128)(2,1)}), bf16[16,8,400]{2,1,0:T(8,128)(2,1)S(1)}, u32[]{:S(2)}, u32[]{:S(2)}) async-start(bf16[16,8,400]{2,1,0:T(8,128)(2,1)} %bitcast_select_fusion), calls=%async_computation | async-start | bytes 262144 | tf_op jit(solution)/shard_map/all_to_all | solution.py:81
  18.9 4.6 %collective-permute-start.5 = (s32[1026]{0:T(1024)S(1)}, s32[1026]{0:T(1024)S(1)}, u32[]{:S(2)}, u32[]{:S(2)}) collective-permute-start(s32[1026]{0:T(1024)S(1)} %concatenate.36), channel_id=1, source_target_pairs={{0,28},{2,30},{4,0},{6,2},{8,4},{10,6},{12,8},{14,10},{16,12},{18,... | collective-permute-start | bytes 12320 | tf_op jit(solution)/shard_map/ppermute | solution.py:12
  30.6 1.9 broadcast_select_fusion.6
  32.5 1.8 broadcast_select_fusion.4
  34.2 1.8 broadcast_select_fusion.3
  36.0 1.8 broadcast_select_fusion.1
  40.6 1.9 broadcast_select_fusion.7
  44.3 1.8 broadcast_select_fusion.5
  47.9 1.8 broadcast_select_fusion.2
  52.4 3.7 %collective-permute-start = (bf16[256,400]{0,1:T(8,128)(2,1)S(1)}, bf16[256,400]{0,1:T(8,128)(2,1)S(1)}, u32[]{:S(2)}, u32[]{:S(2)}) collective-permute-start(bf16[256,400]{0,1:T(8,128)(2,1)S(1)} %fusion.26), channel_id=1, source_target_pairs={{0,28},{2,30},{4,0},{6,2},{8,4},{10,6},{12,8},{14,10},{16,12},{18,... | collective-permute-start | bytes 614408 | tf_op jit(solution)/shard_map/ppermute | solution.py:12
  56.1 1.8 broadcast_select_fusion
  61.2 3.2 gather_fusion.18
  66.3 1.9 gather_fusion.20
  68.2 2.6 gather_fusion.21
  74.7 1.9 gather_fusion.23
  76.6 2.6 gather_fusion.24
  81.2 1.9 gather_fusion.26
  83.1 2.6 gather_fusion.27
  86.5 2.0 gather_fusion.3
  91.2 2.0 divide_multiply_fusion.8
  93.2 1.5 fusion.44
  97.5 2.5 scatter_custom_fusion
  100.0 2.6 scatter_custom_fusion.1
  103.2 1.6 convolution_multiply_fusion.6
  104.8 1.5 copy.89
  106.3 3.8 %scatter_fusion = f32[256,400]{1,0:T(8,128)S(1)} fusion(f32[256,400]{1,0:T(8,128)S(1)} %scatter_custom_fusion.1, s32[512]{0:T(512)S(1)} %compare_select_fusion.24, f32[512,400]{1,0:T(8,128)S(1)} %copy.89), kind=kCustom, calls=%fused_computation.30 | custom fusion | flops 204800 | bytes 2459648 | tf_op jit(solution)/shard_map/scatter-add | solution.py:51
  111.7 2.0 gather_fusion.6
  117.3 1.9 divide_multiply_fusion.6
  122.3 1.4 gather_fusion.19
  125.2 2.4 scatter_custom_fusion.4
  128.0 1.6 convolution_multiply_fusion.5
  129.5 1.5 copy.94
  131.0 2.3 scatter_fusion.1
  133.3 3.8 %scatter_fusion.2 = f32[256,400]{1,0:T(8,128)S(1)} fusion(f32[256,400]{1,0:T(8,128)S(1)} %scatter_custom_fusion.4, s32[512]{0:T(512)S(1)} %compare_select_fusion.23, f32[512,400]{1,0:T(8,128)S(1)} %copy.94), kind=kCustom, calls=%fused_computation.33 | custom fusion | flops 204800 | bytes 2459648 | tf_op jit(solution)/shard_map/scatter-add | solution.py:51
  139.6 2.0 gather_fusion.9
  144.3 1.8 broadcast_multiply_fusion
  146.7 1.5 fusion.50
  148.6 2.3 scatter_custom_fusion.7
  151.1 2.3 convolution_multiply_fusion.4
  153.4 1.5 copy.97
  154.9 2.3 scatter_fusion.3
  157.2 4.2 %scatter_fusion.4 = f32[256,400]{1,0:T(8,128)S(1)} fusion(f32[256,400]{1,0:T(8,128)S(1)} %scatter_custom_fusion.7, s32[512]{0:T(512)S(1)} %bitcast.232, f32[512,400]{1,0:T(8,128)S(1)} %copy.97), kind=kCustom, calls=%fused_computation.36 | custom fusion | flops 204800 | bytes 2459648 | tf_op jit(solution)/shard_map/scatter-add | solution.py:51
  162.3 2.0 gather_fusion.12
  167.2 1.8 divide_multiply_fusion.3
  172.0 1.4 gather_fusion.22
  174.9 2.4 scatter_custom_fusion.10
  177.5 1.6 convolution_multiply_fusion.3
  179.0 1.5 copy.102
  180.5 2.3 scatter_fusion.5
  182.8 4.0 %scatter_fusion.6 = f32[256,400]{1,0:T(8,128)S(1)} fusion(f32[256,400]{1,0:T(8,128)S(1)} %scatter_custom_fusion.10, s32[512]{0:T(512)S(1)} %compare_select_fusion.22, f32[512,400]{1,0:T(8,128)S(1)} %copy.102), kind=kCustom, calls=%fused_computation.39 | custom fusion | flops 204800 | bytes 2459648 | tf_op jit(solution)/shard_map/scatter-add | solution.py:51
  188.7 2.0 gather_fusion.15
  193.5 1.9 divide_multiply_fusion.1
  196.7 1.4 gather_fusion.25
  199.6 2.4 scatter_custom_fusion.13
  202.1 1.6 convolution_multiply_fusion.2
  203.6 1.5 copy.107
  205.1 2.3 scatter_fusion.7
  207.5 4.0 %scatter_fusion.8 = f32[256,400]{1,0:T(8,128)S(1)} fusion(f32[256,400]{1,0:T(8,128)S(1)} %scatter_custom_fusion.13, s32[512]{0:T(512)S(1)} %copy-done.30, f32[512,400]{1,0:T(8,128)S(1)} %copy.107), kind=kCustom, calls=%fused_computation.42 | custom fusion | flops 204800 | bytes 2459648 | tf_op jit(solution)/shard_map/scatter-add | solution.py:51
  212.3 17.3 %all-reduce.6 = (f32[]{:T(128)}, bf16[256,400]{1,0:T(8,128)(2,1)S(1)}) all-reduce(f32[]{:T(128)S(6)} %add.576, f32[256,400]{1,0:T(8,128)S(1)} %add.616), channel_id=1, replica_groups=mesh['dom'=16,'rep'=2] {'rep'}, use_global_device_ids=true, to_apply=%region_15.17 | all-reduce | flops 102401 | bytes 614408 | tf_op jit(solution)/shard_map/psum | solution.py:135
  234.9 8.7 %all-to-all-start.1 = ((bf16[16,8,400]{2,1,0:T(8,128)(2,1)}), bf16[16,8,400]{2,1,0:T(8,128)(2,1)S(1)}, u32[]{:S(2)}, u32[]{:S(2)}) async-start(bf16[16,8,400]{2,1,0:T(8,128)(2,1)} %bitcast.76), calls=%async_computation.1 | async-start | bytes 262144 | tf_op jit(solution)/shard_map/all_to_all | solution.py:150
  243.6 35.0 %psum.36 = f32[]{:T(128)} all-reduce(f32[]{:T(128)} %get-tuple-element.96), channel_id=1, replica_groups=mesh['dom'=16,'rep'=2] {'dom'}, use_global_device_ids=true, to_apply=%region_16.18 | all-reduce | flops 1 | bytes 8 | tf_op jit(solution)/shard_map/psum | solution.py:173
  279.8 1.6 scatter_custom_fusion.15
  282.3 50.7 %all-reduce.5.cloned.1.call-done = (f32[400,400]{0,1:T(8,128)}, f32[400,400]{1,0:T(8,128)}) async-done(((f32[400,400]{0,1:T(8,128)}, f32[400,400]{1,0:T(8,128)}), (f32[400,400]{0,1:T(8,128)}, f32[400,400]{1,0:T(8,128)})) %all-reduce.5.cloned.1.call-update) | async-done | bytes 1280016 | tf_op jit(solution)/shard_map/psum | solution.py:173
  333.1 2.4 copy.112
  (350 shorter events, 74.4 us)
Async XLA Ops:
  7.2 44.6 %copy-start = (bf16[400,400]{1,0:T(8,128)(2,1)S(1)}, bf16[400,400]{1,0:T(8,128)(2,1)}, u32[]{:S(2)}) copy-start(bf16[400,400]{1,0:T(8,128)(2,1)} %param.33) | copy-start | bytes 960004
  10.1 8.4 %copy-start.26 = (s32[1,5,2]{1,2,0:T(2,128)S(1)}, s32[1,5,2]{1,2,0:T(2,128)}, u32[]{:S(2)}) copy-start(s32[1,5,2]{1,2,0:T(2,128)} %param.40) | copy-start | bytes 124
  10.1 8.6 %copy-start.24 = (s32[1,5,512]{2,0,1:T(1,128)S(1)}, s32[1,5,512]{2,0,1:T(1,128)}, u32[]{:S(2)}) copy-start(s32[1,5,512]{2,0,1:T(1,128)} %param.41) | copy-start | bytes 30724
  10.1 8.6 %copy-start.31 = (s32[1,5,256]{2,0,1:T(1,128)S(1)}, s32[1,5,256]{2,0,1:T(1,128)}, u32[]{:S(2)}) copy-start(s32[1,5,256]{2,0,1:T(1,128)} %param.38) | copy-start | bytes 15364
  10.1 8.6 %copy-start.32 = (s32[1,5,256]{2,0,1:T(1,128)S(1)}, s32[1,5,256]{2,0,1:T(1,128)}, u32[]{:S(2)}) copy-start(s32[1,5,256]{2,0,1:T(1,128)} %param.39) | copy-start | bytes 15364
  10.2 17.2 %copy-start.3 = (bf16[400,400]{1,0:T(8,128)(2,1)S(1)}, bf16[400,400]{1,0:T(8,128)(2,1)}, u32[]{:S(2)}) copy-start(bf16[400,400]{1,0:T(8,128)(2,1)} %param.32) | copy-start | bytes 960004
  10.9 16.4 %copy-start.1 = (bf16[256,400]{0,1:T(8,128)(2,1)S(1)}, bf16[256,400]{0,1:T(8,128)(2,1)}, u32[]{:S(2)}) copy-start(bf16[256,400]{0,1:T(8,128)(2,1)} %param.31) | copy-start | bytes 614404
  10.9 39.4 %all-to-all-start = ((bf16[16,8,400]{2,1,0:T(8,128)(2,1)}), bf16[16,8,400]{2,1,0:T(8,128)(2,1)S(1)}, u32[]{:S(2)}, u32[]{:S(2)}) async-start(bf16[16,8,400]{2,1,0:T(8,128)(2,1)} %bitcast_select_fusion), calls=%async_computation | async-start | bytes 262144 | tf_op jit(solution)/shard_map/all_to_all | solution.py:81
  18.4 314.6 %all-reduce.5.cloned.1.call-start = ((), (), s32[]{:S(2)}) async-start(), calls=%async_computation.2 | async-start | bytes 3276800 | tf_op jit(solution)/shard_map/psum | solution.py:173
  18.9 19.6 %collective-permute-start.5 = (s32[1026]{0:T(1024)S(1)}, s32[1026]{0:T(1024)S(1)}, u32[]{:S(2)}, u32[]{:S(2)}) collective-permute-start(s32[1026]{0:T(1024)S(1)} %concatenate.36), channel_id=1, source_target_pairs={{0,28},{2,30},{4,0},{6,2},{8,4},{10,6},{12,8},{14,10},{16,12},{18,... | collective-permute-start | bytes 12320 | tf_op jit(solution)/shard_map/ppermute | solution.py:12
  23.6 15.0 %collective-permute-start.6 = (s32[1026]{0:T(1024)S(1)}, s32[1026]{0:T(1024)S(1)}, u32[]{:S(2)}, u32[]{:S(2)}) collective-permute-start(s32[1026]{0:T(1024)S(1)} %concatenate.37), channel_id=1, source_target_pairs={{0,30},{2,0},{4,2},{6,4},{8,6},{10,8},{12,10},{14,12},{16,14},{18,... | collective-permute-start | bytes 12320 | tf_op jit(solution)/shard_map/ppermute | solution.py:12
  23.7 15.0 %collective-permute-start.7 = (s32[1026]{0:T(1024)S(1)}, s32[1026]{0:T(1024)S(1)}, u32[]{:S(2)}, u32[]{:S(2)}) collective-permute-start(s32[1026]{0:T(1024)S(1)} %concatenate.38), channel_id=1, source_target_pairs={{0,2},{2,4},{4,6},{6,8},{8,10},{10,12},{12,14},{14,16},{16,18},{18... | collective-permute-start | bytes 12320 | tf_op jit(solution)/shard_map/ppermute | solution.py:12
  24.2 14.5 %collective-permute-start.8 = (s32[1026]{0:T(1024)S(1)}, s32[1026]{0:T(1024)S(1)}, u32[]{:S(2)}, u32[]{:S(2)}) collective-permute-start(s32[1026]{0:T(1024)S(1)} %concatenate.39), channel_id=1, source_target_pairs={{0,4},{2,6},{4,8},{6,10},{8,12},{10,14},{12,16},{14,18},{16,20},{1... | collective-permute-start | bytes 12320 | tf_op jit(solution)/shard_map/ppermute | solution.py:12
  25.2 3.9 %copy-start.34 = (s32[256,1]{0,1:T(1,128)}, s32[256,1]{0,1:T(1,128)S(1)}, u32[]{:S(2)}) copy-start(s32[256,1]{0,1:T(1,128)S(1)} %get-tuple-element.148) | copy-start | bytes 3076
  25.3 3.8 %copy-start.37 = (s32[256,1]{0,1:T(1,128)}, s32[256,1]{0,1:T(1,128)S(1)}, u32[]{:S(2)}) copy-start(s32[256,1]{0,1:T(1,128)S(1)} %get-tuple-element.147) | copy-start | bytes 3076
  27.2 23.2 %copy-start.44 = (s32[256,1]{0,1:T(1,128)}, s32[256,1]{0,1:T(1,128)S(1)}, u32[]{:S(2)}) copy-start(s32[256,1]{0,1:T(1,128)S(1)} %get-tuple-element.100) | copy-start | bytes 3076
  27.2 23.2 %copy-start.46 = (s32[256,1]{0,1:T(1,128)}, s32[256,1]{0,1:T(1,128)S(1)}, u32[]{:S(2)}) copy-start(s32[256,1]{0,1:T(1,128)S(1)} %get-tuple-element.101) | copy-start | bytes 3076
  27.2 23.2 %copy-start.48 = (s32[256,1]{0,1:T(1,128)}, s32[256,1]{0,1:T(1,128)S(1)}, u32[]{:S(2)}) copy-start(s32[256,1]{0,1:T(1,128)S(1)} %get-tuple-element.102) | copy-start | bytes 3076
  27.2 23.2 %copy-start.50 = (s32[256,1]{0,1:T(1,128)}, s32[256,1]{0,1:T(1,128)S(1)}, u32[]{:S(2)}) copy-start(s32[256,1]{0,1:T(1,128)S(1)} %get-tuple-element.103) | copy-start | bytes 3076
  27.2 23.2 %copy-start.52 = (s32[256,1]{0,1:T(1,128)}, s32[256,1]{0,1:T(1,128)S(1)}, u32[]{:S(2)}) copy-start(s32[256,1]{0,1:T(1,128)S(1)} %get-tuple-element.104) | copy-start | bytes 3076
  27.3 23.2 %copy-start.54 = (s32[256,1]{0,1:T(1,128)}, s32[256,1]{0,1:T(1,128)S(1)}, u32[]{:S(2)}) copy-start(s32[256,1]{0,1:T(1,128)S(1)} %get-tuple-element.105) | copy-start | bytes 3076
  27.3 23.2 %copy-start.56 = (s32[256,1]{0,1:T(1,128)}, s32[256,1]{0,1:T(1,128)S(1)}, u32[]{:S(2)}) copy-start(s32[256,1]{0,1:T(1,128)S(1)} %get-tuple-element.106) | copy-start | bytes 3076
  27.3 23.2 %copy-start.58 = (s32[256,1]{0,1:T(1,128)}, s32[256,1]{0,1:T(1,128)S(1)}, u32[]{:S(2)}) copy-start(s32[256,1]{0,1:T(1,128)S(1)} %get-tuple-element.107) | copy-start | bytes 3076
  27.3 23.2 %copy-start.60 = (s32[256,1]{0,1:T(1,128)}, s32[256,1]{0,1:T(1,128)S(1)}, u32[]{:S(2)}) copy-start(s32[256,1]{0,1:T(1,128)S(1)} %get-tuple-element.108) | copy-start | bytes 3076
  27.3 23.2 %copy-start.62 = (s32[256,1]{0,1:T(1,128)}, s32[256,1]{0,1:T(1,128)S(1)}, u32[]{:S(2)}) copy-start(s32[256,1]{0,1:T(1,128)S(1)} %get-tuple-element.109) | copy-start | bytes 3076
  27.3 23.2 %copy-start.75 = (pred[256]{0:T(512)(128)(4,1)}, pred[256]{0:T(512)(128)(4,1)S(1)}, u32[]{:S(2)}) copy-start(pred[256]{0:T(512)(128)(4,1)S(1)} %get-tuple-element.162) | copy-start | bytes 772
  27.4 23.2 %copy-start.77 = (pred[256]{0:T(512)(128)(4,1)}, pred[256]{0:T(512)(128)(4,1)S(1)}, u32[]{:S(2)}) copy-start(pred[256]{0:T(512)(128)(4,1)S(1)} %get-tuple-element.163) | copy-start | bytes 772
  27.4 23.2 %copy-start.79 = (pred[256]{0:T(512)(128)(4,1)}, pred[256]{0:T(512)(128)(4,1)S(1)}, u32[]{:S(2)}) copy-start(pred[256]{0:T(512)(128)(4,1)S(1)} %get-tuple-element.164) | copy-start | bytes 772
  27.4 23.2 %copy-start.81 = (pred[256]{0:T(512)(128)(4,1)}, pred[256]{0:T(512)(128)(4,1)S(1)}, u32[]{:S(2)}) copy-start(pred[256]{0:T(512)(128)(4,1)S(1)} %get-tuple-element.165) | copy-start | bytes 772
  27.4 23.2 %copy-start.83 = (pred[256]{0:T(512)(128)(4,1)}, pred[256]{0:T(512)(128)(4,1)S(1)}, u32[]{:S(2)}) copy-start(pred[256]{0:T(512)(128)(4,1)S(1)} %get-tuple-element.166) | copy-start | bytes 772
  27.4 23.2 %copy-start.85 = (pred[256]{0:T(512)(128)(4,1)}, pred[256]{0:T(512)(128)(4,1)S(1)}, u32[]{:S(2)}) copy-start(pred[256]{0:T(512)(128)(4,1)S(1)} %get-tuple-element.167) | copy-start | bytes 772
  27.4 23.2 %copy-start.87 = (pred[256]{0:T(512)(128)(4,1)}, pred[256]{0:T(512)(128)(4,1)S(1)}, u32[]{:S(2)}) copy-start(pred[256]{0:T(512)(128)(4,1)S(1)} %get-tuple-element.168) | copy-start | bytes 772
  27.4 23.2 %copy-start.89 = (pred[256]{0:T(512)(128)(4,1)}, pred[256]{0:T(512)(128)(4,1)S(1)}, u32[]{:S(2)}) copy-start(pred[256]{0:T(512)(128)(4,1)S(1)} %get-tuple-element.169) | copy-start | bytes 772
  27.4 23.2 %copy-start.91 = (pred[256]{0:T(512)(128)(4,1)}, pred[256]{0:T(512)(128)(4,1)S(1)}, u32[]{:S(2)}) copy-start(pred[256]{0:T(512)(128)(4,1)S(1)} %get-tuple-element.170) | copy-start | bytes 772
  27.4 23.2 %copy-start.93 = (pred[256]{0:T(512)(128)(4,1)}, pred[256]{0:T(512)(128)(4,1)S(1)}, u32[]{:S(2)}) copy-start(pred[256]{0:T(512)(128)(4,1)S(1)} %get-tuple-element.171) | copy-start | bytes 772
  37.8 12.8 %copy-start.64 = (f32[256]{0:T(256)}, f32[256]{0:T(256)S(1)}, u32[]{:S(2)}) copy-start(f32[256]{0:T(256)S(1)} %convert_element_type.180) | copy-start | bytes 3076
  50.3 7.7 %copy-start.39 = (s32[256]{0:T(256)}, s32[256]{0:T(256)S(1)}, u32[]{:S(2)}) copy-start(s32[256]{0:T(256)S(1)} %get-tuple-element.122) | copy-start | bytes 3076
  52.4 33.2 %collective-permute-start = (bf16[256,400]{0,1:T(8,128)(2,1)S(1)}, bf16[256,400]{0,1:T(8,128)(2,1)S(1)}, u32[]{:S(2)}, u32[]{:S(2)}) collective-permute-start(bf16[256,400]{0,1:T(8,128)(2,1)S(1)} %fusion.26), channel_id=1, source_target_pairs={{0,28},{2,30},{4,0},{6,2},{8,4},{10,6},{12,8},{14,10},{16,12},{18,... | collective-permute-start | bytes 614408 | tf_op jit(solution)/shard_map/ppermute | solution.py:12
  73.9 2.7 copy-start.5
  100.0 3.2 copy-start.21
  100.0 3.2 copy-start.73
  102.6 8.0 %collective-permute-start.1 = (bf16[256,400]{0,1:T(8,128)(2,1)S(1)}, bf16[256,400]{0,1:T(8,128)(2,1)}, u32[]{:S(2)}, u32[]{:S(2)}) collective-permute-start(bf16[256,400]{0,1:T(8,128)(2,1)S(1)} %copy-done.23), channel_id=1, source_target_pairs={{0,2},{2,4},{4,6},{6,8},{8,10},{10,12},{12,14},{14,16},{16,18},{18... | collective-permute-start | bytes 614408 | tf_op jit(solution)/shard_map/ppermute | solution.py:12
  116.3 2.9 copy-start.95
  123.9 4.1 %copy-start.20 = (bf16[512,400]{1,0:T(8,128)(2,1)S(1)}, bf16[512,400]{1,0:T(8,128)(2,1)}, u32[]{:S(2)}) copy-start(bf16[512,400]{1,0:T(8,128)(2,1)} %gather_fusion.21) | copy-start | bytes 1228804
  125.2 2.8 copy-start.72
  127.7 10.8 %collective-permute-start.2 = (bf16[256,400]{0,1:T(8,128)(2,1)}, bf16[256,400]{0,1:T(8,128)(2,1)}, u32[]{:S(2)}, u32[]{:S(2)}) collective-permute-start(bf16[256,400]{0,1:T(8,128)(2,1)} %collective-permute-done.1), channel_id=1, source_target_pairs={{0,2},{2,4},{4,6},{6,8},{8,10},{10,12},{12,14},{14,16},{16,18},{18... | collective-permute-start | bytes 614408 | tf_op jit(solution)/shard_map/ppermute | solution.py:12
  151.0 11.2 %collective-permute-start.3 = (bf16[256,400]{0,1:T(8,128)(2,1)}, bf16[256,400]{0,1:T(8,128)(2,1)S(1)}, u32[]{:S(2)}, u32[]{:S(2)}) collective-permute-start(bf16[256,400]{0,1:T(8,128)(2,1)} %collective-permute-done.2), channel_id=1, source_target_pairs={{0,2},{2,4},{4,6},{6,8},{8,10},{10,12},{12,14},{14,16},{16,18},{18... | collective-permute-start | bytes 614408 | tf_op jit(solution)/shard_map/ppermute | solution.py:12
  173.6 3.9 %copy-start.19 = (bf16[512,400]{1,0:T(8,128)(2,1)S(1)}, bf16[512,400]{1,0:T(8,128)(2,1)}, u32[]{:S(2)}) copy-start(bf16[512,400]{1,0:T(8,128)(2,1)} %gather_fusion.24) | copy-start | bytes 1228804
  177.4 10.2 %collective-permute-start.4 = (bf16[256,400]{0,1:T(8,128)(2,1)S(1)}, bf16[256,400]{0,1:T(8,128)(2,1)}, u32[]{:S(2)}, u32[]{:S(2)}) collective-permute-start(bf16[256,400]{0,1:T(8,128)(2,1)S(1)} %collective-permute-done.3), channel_id=1, source_target_pairs={{0,2},{2,4},{4,6},{6,8},{8,10},{10,12},{12,14},{14,16},{16,18},{18... | collective-permute-start | bytes 614408 | tf_op jit(solution)/shard_map/ppermute | solution.py:12
  198.2 3.8 %copy-start.18 = (bf16[512,400]{1,0:T(8,128)(2,1)S(1)}, bf16[512,400]{1,0:T(8,128)(2,1)}, u32[]{:S(2)}) copy-start(bf16[512,400]{1,0:T(8,128)(2,1)} %gather_fusion.27) | copy-start | bytes 1228804
  207.4 4.8 %copy-start.25 = (s32[1,16,8]{2,1,0:T(8,128)S(1)}, s32[1,16,8]{2,1,0:T(8,128)}, u32[]{:S(2)}) copy-start(s32[1,16,8]{2,1,0:T(8,128)} %copy.108) | copy-start | bytes 1540
  212.3 17.3 %copy-start.13 = (bf16[256,400]{0,1:T(8,128)(2,1)S(1)}, bf16[256,400]{0,1:T(8,128)(2,1)}, u32[]{:S(2)}) copy-start(bf16[256,400]{0,1:T(8,128)(2,1)} %copy-done.12) | copy-start | bytes 614404
  229.6 2.6 copy-start.51
  229.6 2.6 copy-start.53
  229.6 2.6 copy-start.55
  229.7 2.6 copy-start.57
  229.7 2.6 copy-start.59
  229.7 2.6 copy-start.61
  229.7 2.6 copy-start.63
  229.7 2.6 copy-start.65
  229.7 2.6 copy-start.78
  232.9 46.9 %copy-start.28 = (pred[16,8]{1,0:T(8,128)(4,1)S(1)}, pred[16,8]{1,0:T(8,128)(4,1)}, u32[]{:S(2)}) copy-start(pred[16,8]{1,0:T(8,128)(4,1)} %copy-done.27) | copy-start | bytes 388
  234.1 44.5 %copy-start.4 = (bf16[400,400]{1,0:T(8,128)(2,1)S(1)}, bf16[400,400]{1,0:T(8,128)(2,1)}, u32[]{:S(2)}) copy-start(bf16[400,400]{1,0:T(8,128)(2,1)} %param.32) | copy-start | bytes 960004
  234.9 44.9 %all-to-all-start.1 = ((bf16[16,8,400]{2,1,0:T(8,128)(2,1)}), bf16[16,8,400]{2,1,0:T(8,128)(2,1)S(1)}, u32[]{:S(2)}, u32[]{:S(2)}) async-start(bf16[16,8,400]{2,1,0:T(8,128)(2,1)} %bitcast.76), calls=%async_computation.1 | async-start | bytes 262144 | tf_op jit(solution)/shard_map/all_to_all | solution.py:150
  (44 other events, 69.4 us)
Sparse Core Ops, SparseCore 0:
  232.3 100.7 all-reduce.4
where the time goes:
time: 351 us; the launch traced here: 345 us
  local copies, waits for them, and re-layouts  86.5 us (25%)
  other arithmetic  81.2 us (23%)
  blocking collectives  52.3 us (15%)
  waiting for transfers between devices  51.3 us (15%)
  starting transfers between devices  27.1 us (8%)
  matrix products  25.1 us (7%)
  between operations  21.2 us (6%)
    psum x1, waiting for transfers between devices, on_device(): lax.psum((self_part, neigh_part, loss_total), 'dom')  50.7 us
    psum x1, blocking collectives, on_device(): lax.psum((self_part, neigh_part, loss_total), 'dom')  35 us
    scatter-add x10, other arithmetic, edge_terms(): jnp.zeros(visitor.shape, jnp.float32).at[targets].add(dst_grad)  32.1 us
    gather x9, local copies, waits for them, and re-layouts, edge_terms(): neg_emb = visitor[negatives]  20.8 us
    psum x1, blocking collectives, on_device(): home_total, loss_total = lax.psum((home, loss_sum), 'rep')  17.3 us
    unnamed x197, local copies, waits for them, and re-layouts  17.2 us
    mul x9, other arithmetic, edge_terms(): live[:, None] * negative_weight * jax.nn.sigmoid(negative)  15.9 us
    gather x14, local copies, waits for them, and re-layouts, edge_terms(): src_emb = own[sources]  13.9 us
  transfers between devices with their start and end apart: 12, of which 2 were waited for; matrix products, arithmetic and copies ran while one was open for 27% of the time, Pallas kernels for 0%

commit v1 on v0

v1 whole, which is shorter than its diff:
```python
import jax
import jax.numpy as jnp
from jax import lax
from jax.sharding import PartitionSpec as P

negative_weight = 0.03125
contract_last = (((1,), (1,)), ((), ()))
contract_first = (((0,), (0,)), ((), ()))


def from_behind(value, axis, steps):
    count = lax.axis_size(axis)
    pairs = [(source, (source + steps) % count) for source in range(count)]
    return lax.ppermute(value, axis, pairs)


def row_hits(rows, picks):
    ids = lax.broadcasted_iota(jnp.int32, (rows, picks.shape[0]), 0)
    return (ids == picks[None, :]).astype(jnp.bfloat16)


def bucket_counts(rows, sources, targets, negatives):
    src_hits = row_hits(rows, sources)
    dst_hits = row_hits(rows, targets)
    edge_count = lax.dot_general(
        src_hits, dst_hits, contract_last, preferred_element_type=jnp.float32
    )
    src_count = jnp.sum(src_hits.astype(jnp.float32), axis=1)
    neg_count = jnp.sum(row_hits(rows, negatives).astype(jnp.float32), axis=1)
    return edge_count, negative_weight * src_count[:, None] * neg_count[None, :]


def score_grad(own, visitor, counts, with_loss):
    edge_count, pair_count = counts
    scale = own.shape[1] ** (-0.5)
    score = (
        lax.dot_general(own, visitor, contract_last, preferred_element_type=jnp.float32) * scale
    )
    decay = jnp.exp(-jnp.abs(score))
    inverse = 1.0 / (1.0 + decay)
    high = inverse
    low = decay * inverse
    sig_pos = jnp.where(score >= 0, high, low)
    sig_neg = jnp.where(score >= 0, low, high)
    grad = ((pair_count * sig_pos - edge_count * sig_neg) * scale).astype(jnp.bfloat16)
    loss = None
    if with_loss:
        shared = jnp.log1p(decay)
        loss = jnp.sum(
            edge_count * (jnp.maximum(-score, 0.0) + shared)
            + pair_count * (jnp.maximum(score, 0.0) + shared)
        )
    return grad, loss


def on_device(
    node_feats,
    w_self,
    w_neigh,
    neighbour_index,
    neighbour_count,
    send_index,
    send_count,
    edge_src,
    edge_dst,
    tile_count,
    neg_rows,
):
    partitions = lax.axis_size("dom")
    replicas = lax.axis_size("rep")
    node_rows, width = node_feats.shape
    fan_out = neighbour_index.shape[1]
    slot_cap = send_index.shape[2]
    window = edge_src.shape[1]
    half_width = (window - 1) // 2
    edge_here = edge_src.shape[2]
    position = jnp.arange(edge_here, dtype=jnp.int32)
    live = position % 128 < jnp.repeat(
        tile_count[0], 128, axis=1, total_repeat_length=edge_here
    )
    live_src = jnp.where(live, edge_src[0], -1)
    packed = jnp.concatenate([live_src, edge_dst[0], neg_rows[0]], axis=1)
    visits = {}
    for offset in range(-half_width, half_width + 1):
        if offset:
            visits[offset] = from_behind(packed[offset + half_width], "dom", offset)
    slot_live = jnp.arange(slot_cap, dtype=jnp.int32)[None, :] < send_count[0][:, None]
    picks = jnp.where(slot_live, send_index[0], -1).reshape(-1)
    send_hits = row_hits(node_rows, picks)
    outgoing = lax.dot_general(
        send_hits, node_feats, contract_first, preferred_element_type=jnp.float32
    ).astype(jnp.bfloat16)
    incoming = lax.all_to_all(outgoing, "dom", split_axis=0, concat_axis=0, tiled=True)
    lookup_table = jnp.concatenate([node_feats, incoming], axis=0)
    columns = jnp.arange(lookup_table.shape[0], dtype=jnp.int32)
    counts_f = neighbour_count.astype(jnp.float32)[:, None]
    adjacency = jnp.zeros((node_rows, lookup_table.shape[0]), jnp.float32)
    for which in range(fan_out):
        hits = (neighbour_index[:, which : which + 1] == columns[None, :]) & (
            which < neighbour_count
        )[:, None]
        adjacency = adjacency + hits.astype(jnp.float32)
    adjacency = adjacency.astype(jnp.bfloat16)
    neighbour_mean = (
        jnp.dot(adjacency, lookup_table, preferred_element_type=jnp.float32) / counts_f
    ).astype(jnp.bfloat16)
    hidden = (
        jnp.dot(node_feats, w_self, preferred_element_type=jnp.float32)
        + jnp.dot(neighbour_mean, w_neigh, preferred_element_type=jnp.float32)
    ).astype(jnp.bfloat16)
    home = jnp.zeros((node_rows, width), jnp.float32)
    loss_sum = jnp.zeros((), jnp.float32)

    def split(row):
        return row[:edge_here], row[edge_here : 2 * edge_here], row[2 * edge_here :]

    for offset in (0, 1, -1, 2, -2):
        own_counts = bucket_counts(node_rows, *split(packed[offset + half_width]))
        visitor = hidden if offset == 0 else from_behind(hidden, "dom", -offset)
        grad, loss = score_grad(hidden, visitor, own_counts, True)
        loss_sum = loss_sum + loss
        home = home + jnp.dot(grad, visitor, preferred_element_type=jnp.float32)
        if offset == 0:
            home = home + lax.dot_general(
                grad, hidden, contract_first, preferred_element_type=jnp.float32
            )
        else:
            back = bucket_counts(node_rows, *split(visits[-offset]))
            back_grad, unused = score_grad(visitor, hidden, back, False)
            home = home + lax.dot_general(
                back_grad, visitor, contract_first, preferred_element_type=jnp.float32
            )
    home_total, loss_total = lax.psum((home, loss_sum), "rep")
    grad_b = home_total.astype(jnp.bfloat16)
    scale = float(node_rows * partitions) ** (-0.5)
    self_part = (
        lax.dot_general(node_feats, grad_b, contract_first, preferred_element_type=jnp.float32)
        * scale
    )
    neigh_part = (
        lax.dot_general(
            neighbour_mean, grad_b, contract_first, preferred_element_type=jnp.float32
        )
        * scale
    )
    grad_self, grad_neigh, loss_all = lax.psum((self_part, neigh_part, loss_total), "dom")
    direct = lax.dot_general(grad_b, w_self, contract_last, preferred_element_type=jnp.float32)
    grad_mean = (
        lax.dot_general(grad_b, w_neigh, contract_last, preferred_element_type=jnp.float32)
        / counts_f
    ).astype(jnp.bfloat16)
    table_grad = lax.dot_general(
        adjacency, grad_mean, contract_first, preferred_element_type=jnp.float32
    )
    returned = lax.all_to_all(
        table_grad[node_rows:].astype(jnp.bfloat16),
        "dom",
        split_axis=0,
        concat_axis=0,
        tiled=True,
    )
    scattered = jnp.dot(send_hits, returned, preferred_element_type=jnp.float32)
    grad_x = direct + table_grad[:node_rows] + scattered
    loss = loss_all / float(partitions * window * edge_here * replicas)
    return (loss, grad_x, grad_self, grad_neigh)


def solution(mesh):
    in_specs = (
        P("dom", None),
        P(),
        P(),
        P("dom", None),
        P("dom"),
        P("dom", None, None),
        P("dom", None),
        P("dom", None, "rep"),
        P("dom", None, "rep"),
        P("dom", None, "rep"),
        P("dom", None, None),
    )
    out_specs = (P(), P("dom", None), P(), P())
    return jax.shard_map(
        on_device, mesh=mesh, in_specs=in_specs, out_specs=out_specs, check_vma=False
    )
```

time: 351 us -> 208 us (0.59); the launches traced: 345 us -> 207 us
  other arithmetic: 81.2 us -> 5.34 us
  local copies, waits for them, and re-layouts: 86.5 us -> 15.7 us
  matrix products: 25.1 us -> 32.6 us
  waiting for transfers between devices: 51.3 us -> 57.1 us
    gather x45 -> x1, local copies, waits for them, and re-layouts: 53.2 us -> 0.73 us  [on_device(): jnp.repeat(tile_count[0], 128, axis=1, total_repeat_length=edge_here)]
    scatter-add x16 -> x0, other arithmetic: 45.5 us -> none  [the longest x10 32.1 us: edge_terms(): jnp.zeros(visitor.shape, jnp.float32).at[targets].add(dst_grad)]
    mul x19 -> x9, other arithmetic: 30.6 us -> 1.18 us  [bucket_counts(): negative_weight * src_count[:, None] * neg_count[None, :]]
    mul x11 -> x0, local copies, waits for them, and re-layouts: 10.5 us -> none  [the longest x5 7.37 us: edge_terms(): scale * lax.dot_general(neg_grad, src_emb, (((0,), (0,)), ((), ())), pref...]
    dot_general x19 -> x30, matrix products: 23.3 us -> 30.8 us  [the longest x9 9.05 us: score_grad(): lax.dot_general(own, visitor, contract_last, preferred_element_type=jnp.f...]
    unnamed x197 -> x142, local copies, waits for them, and re-layouts: 17.2 us -> 10.9 us
    all_to_all x1, starting transfers between devices: 8.7 us -> 3.51 us  [on_device(): lax.all_to_all(table_grad[node_rows:].astype(jnp.bfloat16), 'dom', split_...]
    ppermute x9 -> x8, waiting for transfers between devices: 0.5 us -> 4.96 us  [from_behind(): return lax.ppermute(value, axis, pairs)]
  transfers between devices with their start and end apart: 12 -> 11, of which waited for: 2 -> 2; matrix products, arithmetic and copies ran while one was open for 27% -> 10% of each run, Pallas kernels for 0% -> 0%
where the time goes in v1:
time: 208 us; the launch traced here: 207 us
  waiting for transfers between devices  57.1 us (27%)
  blocking collectives  50.3 us (24%)
  matrix products  32.6 us (16%)
  starting transfers between devices  25.8 us (12%)
  between operations  20 us (10%)
  local copies, waits for them, and re-layouts  15.7 us (8%)
  other arithmetic  5.34 us (3%)
    psum x1, waiting for transfers between devices, on_device(): lax.psum((self_part, neigh_part, loss_total), 'dom')  52.1 us
    psum x1, blocking collectives, on_device(): lax.psum((self_part, neigh_part, loss_total), 'dom')  34.7 us
    psum x1, blocking collectives, on_device(): home_total, loss_total = lax.psum((home, loss_sum), 'rep')  15.6 us
    ppermute x8, starting transfers between devices, from_behind(): return lax.ppermute(value, axis, pairs)  14.9 us
    unnamed x142, local copies, waits for them, and re-layouts  10.9 us
    dot_general x9, matrix products, score_grad(): lax.dot_general(own, visitor, contract_last, preferred_element_type=jnp.f...  9.05 us
    dot_general x4, matrix products, on_device(): lax.dot_general(back_grad, visitor, contract_first, preferred_element_typ...  8.78 us
    all_to_all x1, starting transfers between devices, on_device(): lax.all_to_all(outgoing, 'dom', split_axis=0, concat_axis=0, tiled=True)  7.39 us
  transfers between devices with their start and end apart: 11, of which 2 were waited for; matrix products, arithmetic and copies ran while one was open for 10% of the time, Pallas kernels for 0%

profile of v1, /device:TPU:0, one launch (start us, length us, event | category | flops | bytes accessed | tf_op | source)
XLA Modules:
  0.0 206.8 jit_solution(17418534703793869219)
XLA Ops:
  7.2 0.8 copy.27
  8.1 0.6 copy-done.47
  8.9 1.1 convolution_convert_fusion
  10.1 0.8 copy.28
  10.8 7.4 %all-to-all-start = ((bf16[16,8,400]{2,1,0:T(8,128)(2,1)}), bf16[16,8,400]{2,1,0:T(8,128)(2,1)S(1)}, u32[]{:S(2)}, u32[]{:S(2)}) async-start(bf16[16,8,400]{2,1,0:T(8,128)(2,1)} %bitcast.20), calls=%async_computation | async-start | bytes 262144 | tf_op jit(solution)/shard_map/all_to_all | solution.py:93
  18.4 0.7 copy-done.15
  19.2 0.7 copy-done.1
  19.9 0.7 gather_fusion
  20.8 0.6 copy-done.12
  21.5 4.4 %collective-permute-start.4 = (s32[1024]{0:T(1024)S(1)}, s32[1024]{0:T(1024)S(1)}, u32[]{:S(2)}, u32[]{:S(2)}) collective-permute-start(s32[1024]{0:T(1024)S(1)} %bitcast.112), channel_id=1, source_target_pairs={{0,30},{2,0},{4,2},{6,4},{8,6},{10,8},{12,10},{14,12},{16,14},{18,... | collective-permute-start | bytes 12296 | tf_op jit(solution)/shard_map/ppermute | solution.py:14
  25.9 0.8 collective-permute-start.6
  26.7 1.3 collective-permute-start.7
  27.9 0.4 slice_reduce_fusion
  28.4 0.7 copy-done.14
  29.1 0.7 copy-done.16
  30.0 0.3 fusion.223
  32.9 0.6 fusion.220
  33.6 0.6 broadcast_multiply_fusion.2
  34.1 0.7 convert_reduce_fusion.2
  34.8 0.5 fusion.221
  35.5 0.6 broadcast_multiply_fusion.1
  36.1 0.7 convert_reduce_fusion.1
  36.8 0.6 fusion.222
  37.5 0.7 convert_reduce_fusion
  38.5 1.1 fusion.8
  39.6 0.3 fusion.9
  39.9 0.3 convolution_multiply_fusion.14
  40.2 3.5 %collective-permute-start.2 = (bf16[256,400]{0,1:T(8,128)(2,1)S(1)}, bf16[256,400]{0,1:T(8,128)(2,1)S(1)}, u32[]{:S(2)}, u32[]{:S(2)}) collective-permute-start(bf16[256,400]{0,1:T(8,128)(2,1)S(1)} %fusion.9), channel_id=1, source_target_pairs={{0,28},{2,30},{4,0},{6,2},{8,4},{10,6},{12,8},{14,10},{16,12},{18,... | collective-permute-start | bytes 614408 | tf_op jit(solution)/shard_map/ppermute | solution.py:14
  43.7 3.2 %collective-permute-start = (bf16[256,400]{0,1:T(8,128)(2,1)S(1)}, bf16[256,400]{0,1:T(8,128)(2,1)S(1)}, u32[]{:S(2)}, u32[]{:S(2)}) collective-permute-start(bf16[256,400]{0,1:T(8,128)(2,1)S(1)} %fusion.9), channel_id=1, source_target_pairs={{0,30},{2,0},{4,2},{6,4},{8,6},{10,8},{12,10},{14,12},{16,14},{18,... | collective-permute-start | bytes 614408 | tf_op jit(solution)/shard_map/ppermute | solution.py:14
  47.0 1.7 collective-permute-start.3
  48.6 1.0 fusion.38
  50.1 1.1 fusion.50
  51.1 0.3 fusion.182
  51.5 4.9 %collective-permute-done.1 = bf16[256,400]{0,1:T(8,128)(2,1)S(1)} collective-permute-done((bf16[256,400]{0,1:T(8,128)(2,1)S(1)}, bf16[256,400]{0,1:T(8,128)(2,1)S(1)}, u32[]{:S(2)}, u32[]{:S(2)}) %collective-permute-start.1) | collective-permute-done | bytes 204832 | tf_op jit(solution)/shard_map/ppermute | solution.py:14
  56.4 1.0 convolution_multiply_fusion.7
  57.4 1.0 fusion.45
  58.4 1.3 fusion.184
  59.7 1.0 convolution_multiply_fusion.5
  60.7 1.0 convolution_multiply_fusion.9
  61.7 1.0 convolution_multiply_fusion.3
  62.7 1.0 fusion.55
  63.7 1.1 fusion.180
  64.8 1.8 fusion.40
  66.5 2.2 %fusion.65 = f32[256,400]{0,1:T(8,128)} fusion(bf16[256,400]{0,1:T(8,128)(2,1)S(1)} %collective-permute-done, f32[256,256]{1,0:T(8,128)} %convolution_multiply_fusion.9, s32[256]{0:T(256)S(1)} %get-tuple-element.64, f32[256]{0:T(256)S(1)} %convert_reduce_fusion.3, f32[256]{0:T(256)S(1)} %broadcast_multiply_fusion.3, s32[256]{0:T(256)S(1)} %get-tuple-element.63), kind=kOutput, calls=%fused_computation.146 | convolution fusion | flops 87031808 | bytes 880640 | tf_op jit(solution)/shard_map/dot_general | solution.py:130
  68.8 0.7 copy-done.37
  69.4 2.2 %fusion.71 = f32[256,400]{0,1:T(8,128)} fusion(bf16[256,400]{0,1:T(8,128)(2,1)} %copy-done.11, f32[256,256]{1,0:T(8,128)S(1)} %copy-done.6, s32[256]{0:T(256)S(1)} %copy-done.44, f32[256]{0:T(256)S(1)} %copy-done.37, f32[256]{0:T(256)S(1)} %copy-done.42, s32[256]{0:T(256)S(1)} %get-tuple-element.65), kind=kOutput, calls=%fused_computation.152 | convolution fusion | flops 87031808 | bytes 880640 | tf_op jit(solution)/shard_map/dot_general | solution.py:130
  71.6 0.6 copy-done.38
  72.2 2.2 %fusion.77 = f32[256,400]{0,1:T(8,128)} fusion(bf16[256,400]{0,1:T(8,128)(2,1)S(1)} %copy-done.9, f32[256,256]{1,0:T(8,128)} %convolution_multiply_fusion.5, s32[256]{0:T(256)S(1)} %copy-done.45, f32[256]{0:T(256)S(1)} %copy-done.38, f32[256]{0:T(256)S(1)} %copy-done.43, s32[256]{0:T(256)S(1)} %get-tuple-element.67), kind=kOutput, calls=%fused_computation.158 | convolution fusion | flops 87031808 | bytes 880640 | tf_op jit(solution)/shard_map/dot_general | solution.py:130
  74.4 0.6 copy-done.39
  75.1 2.2 %fusion.83 = f32[256,400]{0,1:T(8,128)} fusion(bf16[256,400]{0,1:T(8,128)(2,1)} %copy-done.10, f32[256,256]{1,0:T(8,128)S(1)} %copy-done.7, s32[256]{0:T(256)S(1)} %copy-done.46, f32[256]{0:T(256)S(1)} %copy-done.39, f32[256]{0:T(256)S(1)} %broadcast_multiply_fusion, s32[256]{0:T(256)S(1)} %get-tuple-element.69), kind=kOutput, calls=%fused_computation.164 | convolution fusion | flops 87031808 | bytes 880640 | tf_op jit(solution)/shard_map/dot_general | solution.py:130
  77.2 2.0 fusion.7
  82.4 15.6 %all-reduce.6 = (f32[]{:T(128)}, bf16[256,400]{0,1:T(8,128)(2,1)S(1)}) all-reduce(f32[]{:T(128)S(6)} %add.246, f32[256,400]{0,1:T(8,128)S(1)} %fusion.7), channel_id=1, replica_groups=mesh['dom'=16,'rep'=2] {'rep'}, use_global_device_ids=true, to_apply=%region_15.16 | all-reduce | flops 102401 | bytes 614408 | tf_op jit(solution)/shard_map/psum | solution.py:133
  98.0 1.2 convolution_multiply_fusion
  99.2 1.2 fusion
  100.5 0.5 copy-done.18
  101.2 1.2 fusion.11
  102.4 0.8 copy.31
  103.2 3.5 %all-to-all-start.1 = ((bf16[16,8,400]{2,1,0:T(8,128)(2,1)}), bf16[16,8,400]{2,1,0:T(8,128)(2,1)S(1)}, u32[]{:S(2)}, u32[]{:S(2)}) async-start(bf16[16,8,400]{2,1,0:T(8,128)(2,1)} %bitcast.35), calls=%async_computation.1 | async-start | bytes 262144 | tf_op jit(solution)/shard_map/all_to_all | solution.py:155
  106.7 34.7 %psum.36 = f32[]{:T(128)} all-reduce(f32[]{:T(128)} %get-tuple-element.35), channel_id=1, replica_groups=mesh['dom'=16,'rep'=2] {'dom'}, use_global_device_ids=true, to_apply=%region_16.17 | all-reduce | flops 1 | bytes 8 | tf_op jit(solution)/shard_map/psum | solution.py:146
  142.0 0.3 convolution_add_fusion.3
  142.3 1.0 convolution_add_fusion.1
  143.3 52.1 %all-reduce.5.cloned.1.call-done = (f32[400,400]{0,1:T(8,128)}, f32[400,400]{1,0:T(8,128)}) async-done(((f32[400,400]{0,1:T(8,128)}, f32[400,400]{1,0:T(8,128)}), (f32[400,400]{0,1:T(8,128)}, f32[400,400]{1,0:T(8,128)})) %all-reduce.5.cloned.1.call-update) | async-done | bytes 1280016 | tf_op jit(solution)/shard_map/psum | solution.py:146
  195.5 2.4 %copy.32 = f32[400,400]{1,0:T(8,128)} copy(f32[400,400]{0,1:T(8,128)} %get-tuple-element.33) | data formatting | bytes 1280000
  197.9 0.9 copy.44
  (195 shorter events, 4.5 us)
Async XLA Ops:
  7.2 32.4 %copy-start = (bf16[400,400]{1,0:T(8,128)(2,1)S(1)}, bf16[400,400]{1,0:T(8,128)(2,1)}, u32[]{:S(2)}) copy-start(bf16[400,400]{1,0:T(8,128)(2,1)} %param.15) | copy-start | bytes 960004
  10.8 27.3 %all-to-all-start = ((bf16[16,8,400]{2,1,0:T(8,128)(2,1)}), bf16[16,8,400]{2,1,0:T(8,128)(2,1)S(1)}, u32[]{:S(2)}, u32[]{:S(2)}) async-start(bf16[16,8,400]{2,1,0:T(8,128)(2,1)} %bitcast.20), calls=%async_computation | async-start | bytes 262144 | tf_op jit(solution)/shard_map/all_to_all | solution.py:93
  18.2 177.2 %all-reduce.5.cloned.1.call-start = ((), (), s32[]{:S(2)}) async-start(), calls=%async_computation.2 | async-start | bytes 3276800 | tf_op jit(solution)/shard_map/psum | solution.py:146
  18.3 0.7 copy-start.15
  19.2 0.7 copy-start.1
  20.7 0.7 copy-start.12
  20.7 0.7 copy-start.13
  21.4 8.4 %copy-start.3 = (bf16[400,400]{1,0:T(8,128)(2,1)S(1)}, bf16[400,400]{1,0:T(8,128)(2,1)}, u32[]{:S(2)}) copy-start(bf16[400,400]{1,0:T(8,128)(2,1)} %param.14) | copy-start | bytes 960004
  21.5 11.1 %collective-permute-start.4 = (s32[1024]{0:T(1024)S(1)}, s32[1024]{0:T(1024)S(1)}, u32[]{:S(2)}, u32[]{:S(2)}) collective-permute-start(s32[1024]{0:T(1024)S(1)} %bitcast.112), channel_id=1, source_target_pairs={{0,30},{2,0},{4,2},{6,4},{8,6},{10,8},{12,10},{14,12},{16,14},{18,... | collective-permute-start | bytes 12296 | tf_op jit(solution)/shard_map/ppermute | solution.py:14
  25.9 7.0 %collective-permute-start.5 = (s32[1024]{0:T(1024)S(1)}, s32[1024]{0:T(1024)S(1)}, u32[]{:S(2)}, u32[]{:S(2)}) collective-permute-start(s32[1024]{0:T(1024)S(1)} %bitcast.111), channel_id=1, source_target_pairs={{0,2},{2,4},{4,6},{6,8},{8,10},{10,12},{12,14},{14,16},{16,18},{18... | collective-permute-start | bytes 12296 | tf_op jit(solution)/shard_map/ppermute | solution.py:14
  25.9 8.9 %collective-permute-start.6 = (s32[1024]{0:T(1024)S(1)}, s32[1024]{0:T(1024)S(1)}, u32[]{:S(2)}, u32[]{:S(2)}) collective-permute-start(s32[1024]{0:T(1024)S(1)} %bitcast.110), channel_id=1, source_target_pairs={{0,28},{2,30},{4,0},{6,2},{8,4},{10,6},{12,8},{14,10},{16,12},{18,... | collective-permute-start | bytes 12296 | tf_op jit(solution)/shard_map/ppermute | solution.py:14
  26.7 3.2 %copy-start.2 = (bf16[256,400]{0,1:T(8,128)(2,1)S(1)}, bf16[256,400]{0,1:T(8,128)(2,1)}, u32[]{:S(2)}) copy-start(bf16[256,400]{0,1:T(8,128)(2,1)} %param.13) | copy-start | bytes 614404
  26.7 10.1 %collective-permute-start.7 = (s32[1024]{0:T(1024)S(1)}, s32[1024]{0:T(1024)S(1)}, u32[]{:S(2)}, u32[]{:S(2)}) collective-permute-start(s32[1024]{0:T(1024)S(1)} %bitcast.109), channel_id=1, source_target_pairs={{0,4},{2,6},{4,8},{6,10},{8,12},{10,14},{12,16},{14,18},{16,20},{1... | collective-permute-start | bytes 12296 | tf_op jit(solution)/shard_map/ppermute | solution.py:14
  28.3 0.7 copy-start.14
  29.1 0.7 copy-start.16
  29.7 8.5 %copy-start.17 = (s32[256,1]{0,1:T(1,128)}, s32[256,1]{0,1:T(1,128)S(1)}, u32[]{:S(2)}) copy-start(s32[256,1]{0,1:T(1,128)S(1)} %get-tuple-element.43) | copy-start | bytes 3076
  29.7 8.6 %copy-start.19 = (s32[256,1]{0,1:T(1,128)}, s32[256,1]{0,1:T(1,128)S(1)}, u32[]{:S(2)}) copy-start(s32[256,1]{0,1:T(1,128)S(1)} %get-tuple-element.44) | copy-start | bytes 3076
  29.7 8.6 %copy-start.21 = (s32[256,1]{0,1:T(1,128)}, s32[256,1]{0,1:T(1,128)S(1)}, u32[]{:S(2)}) copy-start(s32[256,1]{0,1:T(1,128)S(1)} %get-tuple-element.45) | copy-start | bytes 3076
  29.7 8.6 %copy-start.23 = (s32[256,1]{0,1:T(1,128)}, s32[256,1]{0,1:T(1,128)S(1)}, u32[]{:S(2)}) copy-start(s32[256,1]{0,1:T(1,128)S(1)} %get-tuple-element.46) | copy-start | bytes 3076
  29.8 8.6 %copy-start.25 = (s32[256,1]{0,1:T(1,128)}, s32[256,1]{0,1:T(1,128)S(1)}, u32[]{:S(2)}) copy-start(s32[256,1]{0,1:T(1,128)S(1)} %get-tuple-element.47) | copy-start | bytes 3076
  29.8 8.6 %copy-start.27 = (s32[256,1]{0,1:T(1,128)}, s32[256,1]{0,1:T(1,128)S(1)}, u32[]{:S(2)}) copy-start(s32[256,1]{0,1:T(1,128)S(1)} %get-tuple-element.48) | copy-start | bytes 3076
  29.8 8.6 %copy-start.29 = (s32[256,1]{0,1:T(1,128)}, s32[256,1]{0,1:T(1,128)S(1)}, u32[]{:S(2)}) copy-start(s32[256,1]{0,1:T(1,128)S(1)} %get-tuple-element.49) | copy-start | bytes 3076
  29.8 8.6 %copy-start.31 = (s32[256,1]{0,1:T(1,128)}, s32[256,1]{0,1:T(1,128)S(1)}, u32[]{:S(2)}) copy-start(s32[256,1]{0,1:T(1,128)S(1)} %get-tuple-element.50) | copy-start | bytes 3076
  29.8 8.6 %copy-start.33 = (s32[256,1]{0,1:T(1,128)}, s32[256,1]{0,1:T(1,128)S(1)}, u32[]{:S(2)}) copy-start(s32[256,1]{0,1:T(1,128)S(1)} %get-tuple-element.51) | copy-start | bytes 3076
  29.8 8.6 %copy-start.35 = (s32[256,1]{0,1:T(1,128)}, s32[256,1]{0,1:T(1,128)S(1)}, u32[]{:S(2)}) copy-start(s32[256,1]{0,1:T(1,128)S(1)} %get-tuple-element.52) | copy-start | bytes 3076
  29.9 8.5 %copy-start.48 = (pred[256]{0:T(512)(128)(4,1)}, pred[256]{0:T(512)(128)(4,1)S(1)}, u32[]{:S(2)}) copy-start(pred[256]{0:T(512)(128)(4,1)S(1)} %get-tuple-element.71) | copy-start | bytes 772
  29.9 8.5 %copy-start.50 = (pred[256]{0:T(512)(128)(4,1)}, pred[256]{0:T(512)(128)(4,1)S(1)}, u32[]{:S(2)}) copy-start(pred[256]{0:T(512)(128)(4,1)S(1)} %get-tuple-element.72) | copy-start | bytes 772
  29.9 8.5 %copy-start.52 = (pred[256]{0:T(512)(128)(4,1)}, pred[256]{0:T(512)(128)(4,1)S(1)}, u32[]{:S(2)}) copy-start(pred[256]{0:T(512)(128)(4,1)S(1)} %get-tuple-element.73) | copy-start | bytes 772
  29.9 8.5 %copy-start.54 = (pred[256]{0:T(512)(128)(4,1)}, pred[256]{0:T(512)(128)(4,1)S(1)}, u32[]{:S(2)}) copy-start(pred[256]{0:T(512)(128)(4,1)S(1)} %get-tuple-element.74) | copy-start | bytes 772
  29.9 8.5 %copy-start.56 = (pred[256]{0:T(512)(128)(4,1)}, pred[256]{0:T(512)(128)(4,1)S(1)}, u32[]{:S(2)}) copy-start(pred[256]{0:T(512)(128)(4,1)S(1)} %get-tuple-element.75) | copy-start | bytes 772
  29.9 8.5 %copy-start.58 = (pred[256]{0:T(512)(128)(4,1)}, pred[256]{0:T(512)(128)(4,1)S(1)}, u32[]{:S(2)}) copy-start(pred[256]{0:T(512)(128)(4,1)S(1)} %get-tuple-element.76) | copy-start | bytes 772
  29.9 8.5 %copy-start.60 = (pred[256]{0:T(512)(128)(4,1)}, pred[256]{0:T(512)(128)(4,1)S(1)}, u32[]{:S(2)}) copy-start(pred[256]{0:T(512)(128)(4,1)S(1)} %get-tuple-element.77) | copy-start | bytes 772
  29.9 8.5 %copy-start.62 = (pred[256]{0:T(512)(128)(4,1)}, pred[256]{0:T(512)(128)(4,1)S(1)}, u32[]{:S(2)}) copy-start(pred[256]{0:T(512)(128)(4,1)S(1)} %get-tuple-element.78) | copy-start | bytes 772
  29.9 8.5 %copy-start.64 = (pred[256]{0:T(512)(128)(4,1)}, pred[256]{0:T(512)(128)(4,1)S(1)}, u32[]{:S(2)}) copy-start(pred[256]{0:T(512)(128)(4,1)S(1)} %get-tuple-element.79) | copy-start | bytes 772
  29.9 8.5 %copy-start.66 = (pred[256]{0:T(512)(128)(4,1)}, pred[256]{0:T(512)(128)(4,1)S(1)}, u32[]{:S(2)}) copy-start(pred[256]{0:T(512)(128)(4,1)S(1)} %get-tuple-element.80) | copy-start | bytes 772
  31.4 26.0 %copy-start.5 = (f32[256,256]{1,0:T(8,128)}, f32[256,256]{1,0:T(8,128)S(1)}, u32[]{:S(2)}) copy-start(f32[256,256]{1,0:T(8,128)S(1)} %fusion.117) | copy-start | bytes 786436
  32.6 5.9 %copy-start.40 = (f32[256]{0:T(256)}, f32[256]{0:T(256)S(1)}, u32[]{:S(2)}) copy-start(f32[256]{0:T(256)S(1)} %convert_element_type.209) | copy-start | bytes 3076
  40.2 9.9 %collective-permute-start.2 = (bf16[256,400]{0,1:T(8,128)(2,1)S(1)}, bf16[256,400]{0,1:T(8,128)(2,1)S(1)}, u32[]{:S(2)}, u32[]{:S(2)}) collective-permute-start(bf16[256,400]{0,1:T(8,128)(2,1)S(1)} %fusion.9), channel_id=1, source_target_pairs={{0,28},{2,30},{4,0},{6,2},{8,4},{10,6},{12,8},{14,10},{16,12},{18,... | collective-permute-start | bytes 614408 | tf_op jit(solution)/shard_map/ppermute | solution.py:14
  43.7 17.0 %collective-permute-start = (bf16[256,400]{0,1:T(8,128)(2,1)S(1)}, bf16[256,400]{0,1:T(8,128)(2,1)S(1)}, u32[]{:S(2)}, u32[]{:S(2)}) collective-permute-start(bf16[256,400]{0,1:T(8,128)(2,1)S(1)} %fusion.9), channel_id=1, source_target_pairs={{0,30},{2,0},{4,2},{6,4},{8,6},{10,8},{12,10},{14,12},{16,14},{18,... | collective-permute-start | bytes 614408 | tf_op jit(solution)/shard_map/ppermute | solution.py:14
  46.9 9.5 %collective-permute-start.1 = (bf16[256,400]{0,1:T(8,128)(2,1)S(1)}, bf16[256,400]{0,1:T(8,128)(2,1)S(1)}, u32[]{:S(2)}, u32[]{:S(2)}) collective-permute-start(bf16[256,400]{0,1:T(8,128)(2,1)S(1)} %fusion.9), channel_id=1, source_target_pairs={{0,2},{2,4},{4,6},{6,8},{8,10},{10,12},{12,14},{14,16},{16,18},{18... | collective-permute-start | bytes 614408 | tf_op jit(solution)/shard_map/ppermute | solution.py:14
  47.0 14.7 %collective-permute-start.3 = (bf16[256,400]{0,1:T(8,128)(2,1)S(1)}, bf16[256,400]{0,1:T(8,128)(2,1)S(1)}, u32[]{:S(2)}, u32[]{:S(2)}) collective-permute-start(bf16[256,400]{0,1:T(8,128)(2,1)S(1)} %fusion.9), channel_id=1, source_target_pairs={{0,4},{2,6},{4,8},{6,10},{8,12},{10,14},{12,16},{14,18},{16,20},{1... | collective-permute-start | bytes 614408 | tf_op jit(solution)/shard_map/ppermute | solution.py:14
  50.1 9.6 %copy-start.8 = (bf16[256,400]{0,1:T(8,128)(2,1)}, bf16[256,400]{0,1:T(8,128)(2,1)S(1)}, u32[]{:S(2)}) copy-start(bf16[256,400]{0,1:T(8,128)(2,1)S(1)} %collective-permute-done.2) | copy-start | bytes 614404
  56.4 2.0 copy-start.11
  61.7 2.0 copy-start.10
  66.5 2.2 %copy-start.6 = (f32[256,256]{1,0:T(8,128)S(1)}, f32[256,256]{1,0:T(8,128)}, u32[]{:S(2)}) copy-start(f32[256,256]{1,0:T(8,128)} %convolution_multiply_fusion.7) | copy-start | bytes 786436
  66.5 2.2 %copy-start.42 = (f32[256]{0:T(256)S(1)}, f32[256]{0:T(256)}, u32[]{:S(2)}) copy-start(f32[256]{0:T(256)} %broadcast_multiply_fusion.2) | copy-start | bytes 3076
  66.5 2.2 %copy-start.44 = (s32[256]{0:T(256)S(1)}, s32[256]{0:T(256)}, u32[]{:S(2)}) copy-start(s32[256]{0:T(256)} %get-tuple-element.66) | copy-start | bytes 3076
  69.4 2.2 %copy-start.9 = (bf16[256,400]{0,1:T(8,128)(2,1)S(1)}, bf16[256,400]{0,1:T(8,128)(2,1)}, u32[]{:S(2)}) copy-start(bf16[256,400]{0,1:T(8,128)(2,1)} %copy-done.8) | copy-start | bytes 614404
  69.4 2.2 %copy-start.43 = (f32[256]{0:T(256)S(1)}, f32[256]{0:T(256)}, u32[]{:S(2)}) copy-start(f32[256]{0:T(256)} %broadcast_multiply_fusion.1) | copy-start | bytes 3076
  69.4 2.2 %copy-start.45 = (s32[256]{0:T(256)S(1)}, s32[256]{0:T(256)}, u32[]{:S(2)}) copy-start(s32[256]{0:T(256)} %get-tuple-element.68) | copy-start | bytes 3076
  72.2 2.2 %copy-start.7 = (f32[256,256]{1,0:T(8,128)S(1)}, f32[256,256]{1,0:T(8,128)}, u32[]{:S(2)}) copy-start(f32[256,256]{1,0:T(8,128)} %convolution_multiply_fusion.3) | copy-start | bytes 786436
  72.2 2.2 %copy-start.46 = (s32[256]{0:T(256)S(1)}, s32[256]{0:T(256)}, u32[]{:S(2)}) copy-start(s32[256]{0:T(256)} %get-tuple-element.70) | copy-start | bytes 3076
  100.3 0.7 copy-start.20
  100.3 0.7 copy-start.22
  100.4 0.7 copy-start.24
  100.4 0.7 copy-start.28
  100.4 0.7 copy-start.30
  100.4 0.7 copy-start.32
  100.4 0.7 copy-start.34
  100.4 0.7 copy-start.36
  100.5 0.7 copy-start.63
  100.5 0.7 copy-start.67
  103.2 39.1 %all-to-all-start.1 = ((bf16[16,8,400]{2,1,0:T(8,128)(2,1)}), bf16[16,8,400]{2,1,0:T(8,128)(2,1)S(1)}, u32[]{:S(2)}, u32[]{:S(2)}) async-start(bf16[16,8,400]{2,1,0:T(8,128)(2,1)} %bitcast.35), calls=%async_computation.1 | async-start | bytes 262144 | tf_op jit(solution)/shard_map/all_to_all | solution.py:155
  195.5 2.4 %copy-start.4 = (f32[400,400]{1,0:T(8,128)S(1)}, f32[400,400]{1,0:T(8,128)}, u32[]{:S(2)}) copy-start(f32[400,400]{1,0:T(8,128)} %get-tuple-element.92) | copy-start | bytes 1920004
  (15 other events, 9.9 us)
Sparse Core Ops, SparseCore 0:
  100.7 94.7 all-reduce.4

commit v2 on v1

v2 whole, which is shorter than its diff:
```python
import functools

import jax
import jax.numpy as jnp
from jax import lax
from jax.experimental import pallas as pl
from jax.experimental.pallas import tpu as pltpu
from jax.sharding import PartitionSpec as P

negative_weight = 0.03125
F32 = jnp.float32
BF16 = jnp.bfloat16
MESH = pl.DeviceIdType.MESH


def dot_nn(a, b):
    return lax.dot_general(a, b, (((1,), (0,)), ((), ())), preferred_element_type=F32)


def dot_nt(a, b):
    return lax.dot_general(a, b, (((1,), (1,)), ((), ())), preferred_element_type=F32)


def dot_tn(a, b):
    return lax.dot_general(a, b, (((0,), (0,)), ((), ())), preferred_element_type=F32)


def row_hits(rows, picks):
    ids = lax.broadcasted_iota(jnp.int32, (rows, picks.shape[1]), 0)
    return jnp.where(ids == picks, 1.0, 0.0).astype(F32)


def step_kernel(
    parts,
    neg_parts,
    feats,
    w_self,
    w_neigh,
    nidx,
    nidx_t,
    count_f,
    pick_row,
    pick_col,
    packed,
    loss_out,
    gx_out,
    gs_out,
    gn_out,
    bnd_out,
    bnd_in,
    ret_out,
    ret_in,
    other,
    back,
    hid,
    vis,
    edge_own,
    edge_all,
    pair_own,
    pair_all,
    adj,
    adj_t,
    mean,
    lhs,
    rs_out,
    rs_in,
    full,
    loss_buf,
    home,
    bnd_s,
    bnd_r,
    ret_s,
    ret_r,
    mir_s,
    mir_r,
    idx_s,
    idx_r,
    hid_s,
    hid_r,
    rs_s,
    rs_r,
    ag_s,
    ag_r,
    fwd_s,
    fwd_r,
    los_s,
    los_r,
):
    me = lax.axis_index("dom")
    rep = lax.axis_index("rep")
    rows, width = feats.shape
    fan_out = nidx.shape[1]
    window, _, edge_here = packed.shape
    half = (window - 1) // 2
    owners, chunk = rs_out.shape[0], rs_out.shape[1]
    table = adj.shape[1]
    scale = width ** (-0.5)
    offsets = [o for o in range(-half, half + 1) if o]

    def at(shift):
        return lax.rem(me + shift + parts, parts)

    def copy(src, dst, s, r, dom, replica):
        return pltpu.make_async_remote_copy(
            src_ref=src,
            dst_ref=dst,
            send_sem=s,
            recv_sem=r,
            device_id=(dom, replica),
            device_id_type=MESH,
        )

    barrier = pltpu.get_barrier_semaphore()

    def greet(k, carry):
        pl.semaphore_signal(
            barrier, inc=1, device_id=(at(k), rep), device_id_type=MESH
        )
        return carry

    lax.fori_loop(1, parts, greet, 0)
    for o in range(-half, half + 1):
        pl.semaphore_signal(
            barrier, inc=1, device_id=(at(o), 1 - rep), device_id_type=MESH
        )

    lane = lax.broadcasted_iota(jnp.int32, (pick_col.shape[0], rows), 1)
    gather = jnp.where(lane == pick_col[...], 1.0, 0.0).astype(F32).astype(BF16)
    bnd_out[...] = dot_nn(gather, feats[...]).reshape(bnd_out.shape).astype(BF16)
    bnd_in[me] = bnd_out[me]

    pl.semaphore_wait(barrier, parts - 1 + window)

    def all_send(src_of, dst, s, r, limit=None):
        def send(k, carry):
            peer = at(k)

            def go():
                copy(src_of(peer), dst.at[me], s.at[peer], r.at[me], peer, rep).start()

            if limit is None:
                go()
            else:
                pl.when(peer < limit)(go)
            return carry

        lax.fori_loop(1, parts, send, 0)

    def all_recv(src_of, dst, s, r):
        def take(k, carry):
            peer = at(k)
            copy(src_of(peer), dst.at[peer], s.at[peer], r.at[peer], peer, rep).wait_recv()
            return carry

        lax.fori_loop(1, parts, take, 0)

    def all_done(src_of, dst, s, r, limit=None):
        def done(k, carry):
            peer = at(k)

            def go():
                copy(src_of(peer), dst.at[me], s.at[peer], r.at[me], peer, rep).wait_send()

            if limit is None:
                go()
            else:
                pl.when(peer < limit)(go)
            return carry

        lax.fori_loop(1, parts, done, 0)

    all_send(lambda k: bnd_out.at[k], bnd_in, bnd_s, bnd_r)
    mirror = copy(packed, other, mir_s, mir_r, me, 1 - rep)
    mirror.start()
    idx_copies = []
    for n, o in enumerate(offsets):
        for to in range(2):
            replica = rep if to == 0 else 1 - rep
            idx_copies.append(
                (
                    copy(
                        packed.at[o + half],
                        back.at[o + half, to],
                        idx_s.at[n, to],
                        idx_r.at[n, to],
                        at(o),
                        replica,
                    )
                )
            )
            idx_copies[-1].start()

    col_ids = lax.broadcasted_iota(jnp.int32, (rows, table), 1)
    total = jnp.zeros((rows, table), F32)
    for f in range(fan_out):
        total = total + jnp.where(col_ids == nidx[:, f : f + 1], 1.0, 0.0)
    adj[...] = total.astype(BF16)

    all_recv(lambda k: bnd_out.at[k], bnd_in, bnd_s, bnd_r)
    incoming = bnd_in[...].astype(F32).reshape(table - rows, width).astype(BF16)
    summed = dot_nn(adj[:, :rows], feats[...]) + dot_nn(adj[:, rows:], incoming)
    mean[...] = (summed / count_f[...]).astype(BF16)
    hid[...] = (dot_nn(feats[...], w_self[...]) + dot_nn(mean[...], w_neigh[...])).astype(BF16)
    hid_copies = {}
    for o in sorted(offsets, key=abs):
        w = o + half
        hid_copies[w] = copy(hid, vis.at[w], hid_s.at[w], hid_r.at[w], at(-o), rep)
        hid_copies[w].start()

    row_ids = lax.broadcasted_iota(jnp.int32, (table, rows), 0)
    total_t = jnp.zeros((table, rows), F32)
    for f in range(fan_out):
        total_t = total_t + jnp.where(row_ids == nidx_t[f : f + 1, :], 1.0, 0.0)
    adj_t[...] = total_t.astype(BF16)

    @pl.when(rep == 0)
    def _():
        lhs[...] = feats[...]

    @pl.when(rep != 0)
    def _():
        lhs[...] = mean[...]

    mirror.wait_recv()
    for c in idx_copies:
        c.wait_recv()
    ones = jnp.ones((8, edge_here), BF16)

    def counts(halves):
        return [
            (
                row_hits(rows, ref[w_, 0:1, :] if t is None else ref[w_, t, 0:1, :]),
                row_hits(rows, ref[w_, 1:2, :] if t is None else ref[w_, t, 1:2, :]),
            )
            for ref, w_, t in halves
        ]

    def neg_hits(ref, w_, t):
        out = []
        for n in range(neg_parts):
            row = ref[w_, 2 + n : 3 + n, :] if t is None else ref[w_, t, 2 + n : 3 + n, :]
            out.append(row_hits(rows, row))
        return out

    for w in range(window):
        o = w - half
        own = counts([(packed, w, None), (other, w, None)])
        if o == 0:
            from_there = own
            there_neg = (packed, w, None)
        else:
            v = window - 1 - w
            from_there = counts([(back, v, 0), (back, v, 1)])
            there_neg = (back, v, 0)
        e_own = jnp.zeros((rows, rows), F32)
        e_back = jnp.zeros((rows, rows), F32)
        c_own = jnp.zeros((rows, 1), F32)
        c_back = jnp.zeros((8, rows), F32)
        for src, dst in own:
            e_own = e_own + dot_nt(src.astype(BF16), dst.astype(BF16))
            c_own = c_own + jnp.sum(src, axis=1, keepdims=True)
        for src, dst in from_there:
            e_back = e_back + dot_nt(dst.astype(BF16), src.astype(BF16))
            c_back = c_back + dot_nt(ones, src.astype(BF16))
        d_own = jnp.zeros((8, rows), F32)
        for hits in neg_hits(packed, w, None):
            d_own = d_own + dot_nt(ones, hits.astype(BF16))
        d_back = jnp.zeros((rows, 1), F32)
        for hits in neg_hits(*there_neg):
            d_back = d_back + jnp.sum(hits, axis=1, keepdims=True)
        p_own = (negative_weight * c_own) * d_own[0:1, :]
        edge_own[w] = e_own
        edge_all[w] = e_own + e_back
        pair_own[w] = p_own
        pair_all[w] = p_own + (negative_weight * d_back) * c_back[0:1, :]

    loss_sum = jnp.zeros((1, 1), F32)
    for n, o in enumerate([0] + sorted(offsets, key=abs)):
        w = o + half
        if o == 0:
            visitor = hid[...]
        else:
            hid_copies[w].wait_recv()
            visitor = vis[w]
        score = dot_nt(hid[...], visitor) * scale
        decay = jnp.exp(-jnp.abs(score))
        inverse = 1.0 / (1.0 + decay)
        low = decay * inverse
        up = score >= 0
        sig_pos = jnp.where(up, inverse, low)
        sig_neg = jnp.where(up, low, inverse)
        grad = ((pair_all[w] * sig_pos - edge_all[w] * sig_neg) * scale).astype(BF16)
        shared = jnp.log1p(decay)
        terms = edge_own[w] * (jnp.maximum(-score, 0.0) + shared) + pair_own[w] * (
            jnp.maximum(score, 0.0) + shared
        )
        loss_sum = loss_sum + jnp.sum(
            jnp.sum(terms, axis=1, keepdims=True), axis=0, keepdims=True
        )
        add = dot_nn(grad, visitor)
        home[...] = add if n == 0 else home[...] + add

    grad_b = home[...].astype(BF16)
    loss_buf[me] = jnp.broadcast_to(loss_sum, loss_buf.shape[1:])

    weight_scale = float(rows * parts) ** (-0.5)
    part = dot_tn(lhs[...], grad_b) * weight_scale
    for k in range(owners):
        height = min(chunk, width - k * chunk)
        rs_out[k, :height, :] = part[k * chunk : k * chunk + height, :].astype(BF16)
        if height < chunk:
            rs_out[k, height:, :] = jnp.zeros((chunk - height, width), BF16)
    all_send(lambda k: rs_out.at[k], rs_in, rs_s, rs_r, owners)
    all_send(lambda k: loss_buf.at[me], loss_buf, los_s, los_r)

    direct = dot_nt(grad_b, w_self[...])
    grad_mean = (dot_nt(grad_b, w_neigh[...]) / count_f[...]).astype(BF16)
    ret_out[...] = dot_nn(adj_t[rows:, :], grad_mean).reshape(ret_out.shape).astype(BF16)
    ret_in[me] = ret_out[me]
    all_send(lambda k: ret_out.at[k], ret_in, ret_s, ret_r)
    gx_out[...] = direct + dot_nn(adj_t[:rows, :], grad_mean)

    @pl.when(me < owners)
    def _():
        rs_in[me] = rs_out[me]
        all_recv(lambda k: rs_out.at[me], rs_in, rs_s, rs_r)
        acc = lax.fori_loop(
            0,
            parts,
            lambda k, c: c + rs_in[k].astype(F32),
            jnp.zeros((chunk, width), F32),
        )
        full[rep, me] = acc.astype(BF16)

        def send(k, carry):
            peer = at(k)
            piece = full.at[rep, me]
            copy(piece, piece, ag_s.at[peer], ag_r.at[me], peer, rep).start()
            return carry

        lax.fori_loop(1, parts, send, 0)
        piece = full.at[rep, me]
        copy(piece, piece, fwd_s.at[me], fwd_r.at[me], me, 1 - rep).start()

    all_recv(lambda k: ret_out.at[k], ret_in, ret_s, ret_r)
    returned = ret_in[...].astype(F32).reshape(table - rows, width).astype(BF16)
    scatter = row_hits(rows, pick_row[...]).astype(BF16)
    gx_out[...] = gx_out[...] + dot_nn(scatter, returned)

    all_recv(lambda k: loss_buf.at[me], loss_buf, los_s, los_r)
    loss_out[...] = lax.fori_loop(
        0, parts, lambda k, c: c + loss_buf[k], jnp.zeros(loss_out.shape, F32)
    )

    def pass_on(k, carry):
        owner = at(k)

        @pl.when(owner < owners)
        def _():
            piece = full.at[rep, owner]
            copy(piece, piece, ag_s.at[owner], ag_r.at[owner], owner, rep).wait_recv()
            copy(piece, piece, fwd_s.at[owner], fwd_r.at[owner], me, 1 - rep).start()

        return carry

    lax.fori_loop(1, parts, pass_on, 0)

    def land(k, carry):
        piece = full.at[1 - rep, k]
        copy(piece, piece, fwd_s.at[k], fwd_r.at[k], me, 1 - rep).wait_recv()
        return carry

    lax.fori_loop(0, owners, land, 0)
    for k in range(owners):
        height = min(chunk, width - k * chunk)
        gs_out[k * chunk : k * chunk + height, :] = full[0, k, :height, :].astype(F32)
        gn_out[k * chunk : k * chunk + height, :] = full[1, k, :height, :].astype(F32)

    all_done(lambda k: bnd_out.at[k], bnd_in, bnd_s, bnd_r)
    all_done(lambda k: ret_out.at[k], ret_in, ret_s, ret_r)
    all_done(lambda k: rs_out.at[k], rs_in, rs_s, rs_r, owners)
    all_done(lambda k: loss_buf.at[me], loss_buf, los_s, los_r)
    mirror.wait_send()
    for c in idx_copies:
        c.wait_send()
    for c in hid_copies.values():
        c.wait_send()

    @pl.when(me < owners)
    def _():
        def sent(k, carry):
            peer = at(k)
            piece = full.at[rep, me]
            copy(piece, piece, ag_s.at[peer], ag_r.at[me], peer, rep).wait_send()
            return carry

        lax.fori_loop(1, parts, sent, 0)

    def forwarded(k, carry):
        piece = full.at[rep, k]
        copy(piece, piece, fwd_s.at[k], fwd_r.at[k], me, 1 - rep).wait_send()
        return carry

    lax.fori_loop(0, owners, forwarded, 0)


def on_device(
    node_feats,
    w_self,
    w_neigh,
    neighbour_index,
    neighbour_count,
    send_index,
    send_count,
    edge_src,
    edge_dst,
    tile_count,
    neg_rows,
):
    partitions = lax.axis_size("dom")
    replicas = lax.axis_size("rep")
    node_rows, width = node_feats.shape
    fan_out = neighbour_index.shape[1]
    slot_cap = send_index.shape[2]
    window = edge_src.shape[1]
    edge_here = edge_src.shape[2]
    neg_parts = neg_rows.shape[2] // edge_here
    remote = partitions * slot_cap
    table = node_rows + remote
    position = jnp.arange(edge_here, dtype=jnp.int32)
    filled = jnp.repeat(tile_count[0], 128, axis=1, total_repeat_length=edge_here)
    live_src = jnp.where(position % 128 < filled, edge_src[0], -1)
    packed = jnp.concatenate(
        [
            live_src[:, None],
            edge_dst[0][:, None],
            neg_rows[0].reshape(window, neg_parts, edge_here),
        ],
        axis=1,
    )
    packed = jnp.pad(packed, ((0, 0), (0, -packed.shape[1] % 8), (0, 0)))
    fan = jnp.arange(fan_out, dtype=jnp.int32)[None, :]
    nidx = jnp.where(fan < neighbour_count[:, None], neighbour_index, -1)
    slot_live = jnp.arange(slot_cap, dtype=jnp.int32)[None, :] < send_count[0][:, None]
    picks = jnp.where(slot_live, send_index[0], -1).reshape(-1)
    chunk = -(-width // partitions)
    chunk = -(-chunk // 16) * 16
    owners = -(-width // chunk)
    vmem = pl.BlockSpec(memory_space=pltpu.VMEM)
    dma = pltpu.SemaphoreType.DMA
    outs = pl.pallas_call(
        functools.partial(step_kernel, partitions, neg_parts),
        out_shape=(
            jax.ShapeDtypeStruct((8, 128), F32),
            jax.ShapeDtypeStruct((node_rows, width), F32),
            jax.ShapeDtypeStruct((width, width), F32),
            jax.ShapeDtypeStruct((width, width), F32),
        ),
        in_specs=[vmem] * 9,
        out_specs=(vmem,) * 4,
        scratch_shapes=[
            pltpu.VMEM((partitions, slot_cap, width), BF16),
            pltpu.VMEM((partitions, slot_cap, width), BF16),
            pltpu.VMEM((partitions, slot_cap, width), BF16),
            pltpu.VMEM((partitions, slot_cap, width), BF16),
            pltpu.VMEM(packed.shape, jnp.int32),
            pltpu.VMEM((window, 2) + packed.shape[1:], jnp.int32),
            pltpu.VMEM((node_rows, width), BF16),
            pltpu.VMEM((window, node_rows, width), BF16),
            pltpu.VMEM((window, node_rows, node_rows), F32),
            pltpu.VMEM((window, node_rows, node_rows), F32),
            pltpu.VMEM((window, node_rows, node_rows), F32),
            pltpu.VMEM((window, node_rows, node_rows), F32),
            pltpu.VMEM((node_rows, table), BF16),
            pltpu.VMEM((table, node_rows), BF16),
            pltpu.VMEM((node_rows, width), BF16),
            pltpu.VMEM((node_rows, width), BF16),
            pltpu.VMEM((owners, chunk, width), BF16),
            pltpu.VMEM((partitions, chunk, width), BF16),
            pltpu.VMEM((2, owners, chunk, width), BF16),
            pltpu.VMEM((partitions, 8, 128), F32),
            pltpu.VMEM((node_rows, width), F32),
            dma((partitions,)),
            dma((partitions,)),
            dma((partitions,)),
            dma((partitions,)),
            dma,
            dma,
            dma((window - 1, 2)),
            dma((window - 1, 2)),
            dma((window,)),
            dma((window,)),
            dma((partitions,)),
            dma((partitions,)),
            dma((partitions,)),
            dma((partitions,)),
            dma((owners,)),
            dma((owners,)),
            dma((partitions,)),
            dma((partitions,)),
        ],
        compiler_params=pltpu.CompilerParams(
            collective_id=0, has_side_effects=True, vmem_limit_bytes=48 * 1024 * 1024
        ),
    )(
        node_feats,
        w_self,
        w_neigh,
        nidx,
        nidx.T,
        neighbour_count.astype(F32)[:, None],
        picks[None, :],
        picks[:, None],
        packed,
    )
    loss_tile, grad_x, grad_self, grad_neigh = outs
    loss = loss_tile[0, 0] / float(partitions * window * edge_here * replicas)
    return (loss, grad_x, grad_self, grad_neigh)


def solution(mesh):
    in_specs = (
        P("dom", None),
        P(),
        P(),
        P("dom", None),
        P("dom"),
        P("dom", None, None),
        P("dom", None),
        P("dom", None, "rep"),
        P("dom", None, "rep"),
        P("dom", None, "rep"),
        P("dom", None, None),
    )
    out_specs = (P(), P("dom", None), P(), P())
    return jax.shard_map(
        on_device, mesh=mesh, in_specs=in_specs, out_specs=out_specs, check_vma=False
    )
```

time: 208 us -> 82.3 us (0.40)
  the two profiles are of different devices: /device:TPU:0 before, /device:TPU:13 now
where the time goes in v2:
time: 82.3 us; the launch traced here: 81.8 us
  Pallas kernels  66.8 us (81%)
  local copies, waits for them, and re-layouts  10.9 us (13%)
  between operations  2.6 us (3%)
  other arithmetic  1.44 us (2%)
    pallas_call x1, Pallas kernels, on_device(): pl.pallas_call(functools.partial(step_kernel, partitions, neg_parts), out...  66.8 us
    unnamed x31, local copies, waits for them, and re-layouts  9.01 us

profile of v2, /device:TPU:13, one launch (start us, length us, event | category | flops | bytes accessed | tf_op | source)
XLA Modules:
  0.0 81.8 jit_solution(16248395843948050217)
XLA Ops:
  0.6 0.0 copy-start
  0.6 0.7 copy-done
  1.3 0.0 copy-start.8
  1.3 0.7 copy-done.8
  2.0 0.0 copy-start.12
  2.0 0.6 copy-done.12
  2.7 0.1 iota_compare_fusion.1
  2.8 0.0 copy-start.11
  2.8 0.1 lt.95
  2.9 0.6 copy-done.11
  3.4 0.1 copy.23
  3.5 0.1 squeeze.12
  3.6 0.0 copy-start.7
  3.6 0.1 lt.102
  3.7 0.6 copy-done.7
  4.3 0.0 copy-start.6
  4.4 0.7 copy-done.6
  5.1 0.6 fusion.3.nidx_t
  5.7 0.1 squeeze.16
  5.8 0.6 broadcast_select_fusion.pick_col
  6.4 0.0 copy-start.5
  6.4 0.1 copy.29.nidx
  6.5 0.0 copy-start.9
  6.5 0.0 copy-start.10
  6.5 0.7 gather_fusion
  7.3 0.0 copy-start.1
  7.3 0.0 copy-start.2
  7.3 0.1 copy.27
  7.4 0.0 copy-done.9
  7.4 0.0 copy-done.10
  7.4 0.1 copy.30.count_f
  7.6 0.0 copy-done.5
  7.6 0.1 copy.28.feats
  7.7 0.5 copy-done.1
  8.3 0.1 copy-done.2
  8.4 0.0 copy-start.3
  8.4 0.8 %copy-done.3 = s32[128,1]{1,0:T(8,128)S(1)} copy-done((s32[128,1]{1,0:T(8,128)S(1)}, s32[128,1]{1,0:T(8,128)}, u32[]{:S(2)}) %copy-start.3) | copy-done | bytes 536
  9.3 0.0 copy-start.4
  9.3 0.7 copy-done.4
  10.0 66.8 %shard_map.138 = (f32[8,128]{1,0:T(8,128)S(1)}, f32[256,400]{1,0:T(8,128)S(1)}, f32[400,400]{1,0:T(8,128)S(1)}, f32[400,400]{1,0:T(8,128)S(1)}) custom-call(bf16[256,400]{1,0:T(8,128)(2,1)S(1)} %copy.28.feats, bf16[400,400]{1,0:T(8,128)(2,1)S(1)} %copy-done.1, bf16[400,400]{1,0:T(8,128)(2,1)S(1)} %copy-done.2, s32[256,10]{1,0:T(8,128)S(1)} %copy.29.nidx, ...), custom_call_target="tpu_custom_call" | custom-call | tf_op jit(solution)/shard_map/pallas_call | solution.py:451
  76.8 0.5 slice.19
  77.9 0.9 %copy.31 = f32[256,400]{0,1:T(8,128)} copy(f32[256,400]{1,0:T(8,128)S(1)} %get-tuple-element.29) | data formatting | bytes 819200
  78.9 0.9 %copy.34 = f32[400,400]{1,0:T(8,128)} copy(f32[400,400]{1,0:T(8,128)S(1)} %get-tuple-element.38) | data formatting | bytes 1280000
  79.7 0.9 %copy.35 = f32[400,400]{1,0:T(8,128)} copy(f32[400,400]{1,0:T(8,128)S(1)} %get-tuple-element.39) | data formatting | bytes 1280000
  (14 shorter events, 0.1 us)
Async XLA Ops:
  0.6 0.7 copy-start
  1.3 0.7 copy-start.8
  2.0 0.7 copy-start.12
  2.8 0.7 copy-start.11
  3.6 0.7 copy-start.7
  4.3 0.7 copy-start.6
  6.4 1.2 %copy-start.5 = (bf16[256,400]{0,1:T(8,128)(2,1)S(1)}, bf16[256,400]{0,1:T(8,128)(2,1)}, u32[]{:S(2)}) copy-start(bf16[256,400]{0,1:T(8,128)(2,1)} %param.13) | copy-start | bytes 614404
  6.5 0.8 %copy-start.9 = (s32[1,5,256]{2,0,1:T(1,128)S(1)}, s32[1,5,256]{2,0,1:T(1,128)}, u32[]{:S(2)}) copy-start(s32[1,5,256]{2,0,1:T(1,128)} %param.20) | copy-start | bytes 15364
  6.5 0.9 %copy-start.10 = (s32[1,5,256]{2,0,1:T(1,128)S(1)}, s32[1,5,256]{2,0,1:T(1,128)}, u32[]{:S(2)}) copy-start(s32[1,5,256]{2,0,1:T(1,128)} %param.21) | copy-start | bytes 15364
  7.3 1.0 %copy-start.1 = (bf16[400,400]{1,0:T(8,128)(2,1)S(1)}, bf16[400,400]{1,0:T(8,128)(2,1)}, u32[]{:S(2)}) copy-start(bf16[400,400]{1,0:T(8,128)(2,1)} %w_self.1) | copy-start | bytes 960004
  7.3 1.1 %copy-start.2 = (bf16[400,400]{1,0:T(8,128)(2,1)S(1)}, bf16[400,400]{1,0:T(8,128)(2,1)}, u32[]{:S(2)}) copy-start(bf16[400,400]{1,0:T(8,128)(2,1)} %w_neigh.1) | copy-start | bytes 960004
  8.4 0.8 %copy-start.3 = (s32[128,1]{1,0:T(8,128)S(1)}, s32[128,1]{1,0:T(8,128)}, u32[]{:S(2)}) copy-start(s32[128,1]{1,0:T(8,128)} %broadcast_select_fusion.pick_col) | copy-start | bytes 1540
  9.3 0.7 copy-start.4
